TPU v7x, 32 devices: a whole 2x2x4 slice. The times are simulated.
32 devices in a mesh: groups: 2 (over x), dom: 2 (over core), seq: 8 (over z, y).
Axes of the slice: x: 2, y: 2, z: 4, core: 2. Of those that a mesh axis runs over, the one named last changes fastest.
Arguments:
- latents: bfloat16 [16, 512, 1536], P(('groups', 'dom'), 'seq'), parts along dimension 0, may hold values from -6 to 6
- queries: bfloat16 [16, 512, 1536], P(('groups', 'dom'), 'seq'), parts along dimension 0, may hold values from -64 to 64
- keys: bfloat16 [16, 512, 1536], P(('groups', 'dom'), 'seq'), parts along dimension 0, may hold values from -64 to 64
- values: bfloat16 [16, 512, 1536], P(('groups', 'dom'), 'seq'), parts along dimension 0, may hold values from -6 to 6
- out_weight: bfloat16 [1536, 1536], replicated, may hold values from -0.15625 to 0.15625
- step_index: int32 [2], P('groups'), parts along dimension 0, may hold values from 1 to 27
- embed_weight: bfloat16 [1536, 1024], P('seq'), may hold values from -0.15625 to 0.15625
- norm_gain: float32 [1024], replicated, may hold values from 0.1 to 1.9
- up_weight: bfloat16 [1024, 4096], P(None, 'seq'), may hold values from -0.1875 to 0.1875
- head_weight: float32 [4096], replicated, may hold values from -0.09375 to 0.09375
- prev_logw: float32 [16], P(('groups', 'dom')), parts along dimension 0, may hold values from -20 to 320
- ancestors: int32 [16], P(('groups', 'dom')), parts along dimension 0, may hold values from 0 to 7
Outputs:
- resampled: bfloat16 [16, 512, 1536], P(('groups', 'dom'), 'seq'), parts along dimension 0
- log_weights: float32 [16], P(('groups', 'dom')), parts along dimension 0
There are 2 independent parts, one for each index of `groups`. A program takes and returns all parts, laid end to end along the dimension named above; an argument that names none is the same for every part. Nothing has to cross between parts.
Inputs may be any that keep to these rules, and one draw needn't show every extreme that they name: `ancestors`: index of a particle of the same group.
All inputs are finite; a program needn't handle non-finite values.
Results may differ from a plain program's by a relative error of at most 0.0014.
Values may be sent and summed in bfloat16 or wider, within the bound.
A program may use at most 128 MiB of HBM per device.

v0:
```python
import functools
import math

import jax
import jax.numpy as jnp
from jax import lax
from jax.experimental import pallas as pl
from jax.experimental.pallas import tpu as pltpu
from jax.sharding import PartitionSpec as P

HEADS = 24
STEPS = 28
LANES = 128
MESH = pl.DeviceIdType.MESH

potential_scale = 4.0
norm_eps = 1e-05


def attend_plain(qb, kb, vb, ob, row, rows, column, head_width):
    cols = pl.ds(column, head_width)
    rescale = math.log2(math.e) / math.sqrt(head_width)
    scores = lax.dot_general(
        qb[pl.ds(row, rows), cols],
        kb[:, cols],
        (((1,), (1,)), ((), ())),
        preferred_element_type=jnp.float32,
    )
    highest = jnp.max(scores, axis=-1, keepdims=True)
    expanded = jnp.exp2((scores - highest) * rescale)
    total = jnp.sum(expanded, axis=-1, keepdims=True)
    mixed = jnp.dot(
        expanded.astype(jnp.bfloat16), vb[:, cols], preferred_element_type=jnp.float32
    )
    ob[pl.ds(row, rows), cols] = (mixed / total).astype(ob.dtype)


def attend_pair(qb, kb, vb, ob, row, rows, column, head_width):
    cols = pl.ds(pl.multiple_of(column, LANES), LANES)
    rescale = math.log2(math.e) / math.sqrt(head_width)
    query = qb[pl.ds(row, rows), cols]
    key = kb[:, cols]
    value = vb[:, cols]
    query_low = lax.broadcasted_iota(jnp.int32, query.shape, 1) < head_width
    value_low = lax.broadcasted_iota(jnp.int32, value.shape, 1) < head_width
    results = []
    for head in range(2):
        own_query = query_low if head == 0 else jnp.logical_not(query_low)
        own_value = value_low if head == 0 else jnp.logical_not(value_low)
        scores = lax.dot_general(
            jnp.where(own_query, query, jnp.zeros_like(query)),
            key,
            (((1,), (1,)), ((), ())),
            preferred_element_type=jnp.float32,
        )
        highest = jnp.max(scores, axis=-1, keepdims=True)
        expanded = jnp.exp2((scores - highest) * rescale).astype(jnp.bfloat16)
        results.append(
            jnp.dot(
                expanded,
                jnp.where(own_value, value, jnp.ones_like(value)),
                preferred_element_type=jnp.float32,
            )
        )
    first, second = results
    low = lax.broadcasted_iota(jnp.int32, first.shape, 1) < head_width
    mixed = jnp.where(low, first, second)
    total = pltpu.roll(jnp.where(low, second, first), head_width, 1)
    ob[pl.ds(row, rows), cols] = (mixed / total).astype(ob.dtype)


def piece(ref, item, groups, cols, start, width):
    if groups == 0:
        return ref.at[item]
    offset = pl.multiple_of((item % groups) * cols + start, LANES)
    return ref.at[item // groups, :, pl.ds(offset, width)]


def attention_kernel(
    n, fan, group_count, dom_count, groups, cols, width, head_width, row_block,
    q_ref, k_ref, v_ref, embed_ref, up_ref, o_ref, embed_full, up_full,
    qb, kb, vb, ob, send_sem, recv_sem, own_sem, back_send, back_recv, back_own,
    shard_own, line_send, line_recv, fan_send, fan_recv, group_send, group_recv, dom_send, dom_recv,
):
    me = lax.axis_index("seq")
    my_group = lax.axis_index("groups")
    my_dom = lax.axis_index("dom")
    share_count = group_count * dom_count
    tokens = q_ref.shape[1]
    total_tokens = n * tokens
    chunks = cols // width
    inputs = ((q_ref, qb), (k_ref, kb), (v_ref, vb))

    barrier = pltpu.get_barrier_semaphore()

    @pl.loop(1, n)
    def _(step):
        pl.semaphore_signal(
            barrier, inc=1, device_id={"seq": lax.rem(me + step, n)}, device_id_type=MESH
        )

    for step in range(1, group_count):
        peer = {"groups": lax.rem(my_group + step, group_count)}
        pl.semaphore_signal(barrier, inc=1, device_id=peer, device_id_type=MESH)
    for step in range(1, dom_count):
        peer = {"dom": lax.rem(my_dom + step, dom_count)}
        pl.semaphore_signal(barrier, inc=1, device_id=peer, device_id_type=MESH)
    pl.semaphore_wait(barrier, n - 1 + group_count - 1 + dom_count - 1)

    embed_rows, embed_cols = embed_ref.shape
    up_rows, up_cols = up_ref.shape
    embed_part = embed_cols // share_count
    up_part = up_rows // share_count

    def share(which, owner, group, dom, own=False):
        part = group * dom_count + dom
        if which == 0:
            columns = pl.ds(pl.multiple_of(part * embed_part, LANES), embed_part)
            if own:
                return embed_ref.at[:, columns]
            return embed_full.at[
                pl.ds(pl.multiple_of(owner * embed_rows, 16), embed_rows), columns
            ]
        rows = pl.ds(pl.multiple_of(part * up_part, 16), up_part)
        if own:
            return up_ref.at[rows, :]
        return up_full.at[rows, pl.ds(pl.multiple_of(owner * up_cols, LANES), up_cols)]

    def shard_copy(which):
        if which == 0:
            target = embed_full.at[pl.ds(pl.multiple_of(me * embed_rows, 16), embed_rows), :]
            return pltpu.make_async_copy(embed_ref, target, shard_own.at[0])
        target = up_full.at[:, pl.ds(pl.multiple_of(me * up_cols, LANES), up_cols)]
        return pltpu.make_async_copy(up_ref, target, shard_own.at[1])

    place = lax.div(me, fan)
    lane = lax.rem(me, fan)
    length = n // fan
    signs = (1, -1)

    def line_copy(which, direction, step, incoming):
        sign = signs[direction]
        origin = place - sign * (step if incoming else step - 1)
        owner = lax.rem(origin + n, length) * fan + lane
        to = lax.rem(place + sign + n, length) * fan + lane
        return pltpu.make_async_remote_copy(
            src_ref=share(which, owner, my_group, my_dom, own=step == 1 and not incoming),
            dst_ref=share(which, owner, my_group, my_dom),
            send_sem=line_send.at[which, direction, step - 1],
            recv_sem=line_recv.at[which, direction, step - 1],
            device_id={"seq": to},
            device_id_type=MESH,
        )

    def receives(direction, step):
        return place >= step if direction == 0 else place + step < length

    def sends(direction, step):
        if direction == 0:
            return jnp.logical_and(place >= step - 1, place + 1 < length)
        return jnp.logical_and(place + step - 1 < length, place >= 1)

    def fan_copy(which, spot, shift, incoming, own=False):
        to = lax.rem(lane + shift, fan)
        source = lax.rem(lane - shift + fan, fan) if incoming else lane
        owner = spot * fan + source
        return pltpu.make_async_remote_copy(
            src_ref=share(which, owner, my_group, my_dom, own=own),
            dst_ref=share(which, owner, my_group, my_dom),
            send_sem=fan_send.at[which, shift, spot],
            recv_sem=fan_recv.at[which, shift, spot],
            device_id={"seq": place * fan + to},
            device_id_type=MESH,
        )

    def group_copy(which, owner, shift, incoming):
        other = lax.rem(my_group + shift, group_count)
        source = lax.rem(my_group - shift + group_count, group_count) if incoming else my_group
        return pltpu.make_async_remote_copy(
            src_ref=share(which, owner, source, my_dom),
            dst_ref=share(which, owner, source, my_dom),
            send_sem=group_send.at[which, shift, owner],
            recv_sem=group_recv.at[which, shift, owner],
            device_id={"groups": other},
            device_id_type=MESH,
        )

    def dom_copy(which, owner, shift, group_shift, incoming):
        other = lax.rem(my_dom + shift, dom_count)
        source = lax.rem(my_dom - shift + dom_count, dom_count) if incoming else my_dom
        group = lax.rem(my_group - group_shift + group_count, group_count)
        return pltpu.make_async_remote_copy(
            src_ref=share(which, owner, group, source),
            dst_ref=share(which, owner, group, source),
            send_sem=dom_send.at[which, shift, group_shift, owner],
            recv_sem=dom_recv.at[which, shift, group_shift, owner],
            device_id={"dom": other},
            device_id_type=MESH,
        )

    def spread(which, owner):
        for shift in range(1, group_count):
            group_copy(which, owner, shift, False).start()
        for shift in range(1, dom_count):
            dom_copy(which, owner, shift, 0, False).start()

    def each_arrival(step, action):
        for direction in range(2):

            @pl.when(receives(direction, step))
            def _(direction=direction):
                for which in range(2):
                    action(which, direction, place - signs[direction] * step)

    def line_start():
        for which in range(2):
            for direction in range(2):

                @pl.when(sends(direction, 1))
                def _(which=which, direction=direction):
                    line_copy(which, direction, 1, False).start()

            for shift in range(1, fan):
                fan_copy(which, place, shift, False, own=True).start()
            shard_copy(which).start()

    def line_step(step):
        def action(which, direction, spot):
            line_copy(which, direction, step, True).wait_recv()
            if step + 1 < length:

                @pl.when(sends(direction, step + 1))
                def _():
                    line_copy(which, direction, step + 1, False).start()

            for shift in range(1, fan):
                fan_copy(which, spot, shift, False).start()
            spread(which, spot * fan + lane)

        each_arrival(step, action)

    def fan_step(step):
        def action(which, direction, spot):
            for shift in range(1, fan):
                fan_copy(which, spot, shift, True).wait_recv()
                spread(which, spot * fan + lax.rem(lane - shift + fan, fan))

        if step == 0:
            for which in range(2):
                action(which, 0, place)
        else:
            each_arrival(step, action)

    def group_block(which, owner):
        for group_shift in range(1, group_count):
            group_copy(which, owner, group_shift, True).wait_recv()
            for shift in range(1, dom_count):
                dom_copy(which, owner, shift, group_shift, False).start()

    def group_step(step):
        def action(which, direction, spot):
            if step > 0:
                group_block(which, spot * fan + lane)
            for shift in range(1, fan):
                group_block(which, spot * fan + lax.rem(lane - shift + fan, fan))

        if step == 0:
            for which in range(2):
                action(which, 0, place)
        else:
            each_arrival(step, action)

    def weight_step(step):
        if 1 <= step < length:
            line_step(step)
        if 0 <= step - 1 < length:
            fan_step(step - 1)
        if 0 <= step - 2 < length:
            group_step(step - 2)

    weight_steps = length + 2

    def finish_weights():
        for which in range(2):
            shard_copy(which).wait()
            for direction in range(2):
                for step in range(1, length):

                    @pl.when(sends(direction, step))
                    def _(which=which, direction=direction, step=step):
                        line_copy(which, direction, step, False).wait_send()

            @pl.loop(0, length)
            def _(spot, which=which):
                for shift in range(1, fan):
                    fan_copy(which, spot, shift, False).wait_send()

            @pl.loop(1, n)
            def _(step, which=which):
                owner = lax.rem(me + step, n)
                for shift in range(1, group_count):
                    group_copy(which, owner, shift, False).wait_send()
                for shift in range(1, dom_count):
                    for group_shift in range(group_count):
                        dom_copy(which, owner, shift, group_shift, True).wait_recv()
                        dom_copy(which, owner, shift, group_shift, False).wait_send()

    def rows_of(ref, owner, chunk):
        row = pl.ds(pl.multiple_of(owner * tokens, 16), tokens)
        return ref.at[row, pl.ds(chunk * width, width)]

    def outgoing(index, chunk, target, slot):
        source, buffer = inputs[index]
        return pltpu.make_async_remote_copy(
            src_ref=piece(source, target, groups, cols, chunk * width, width),
            dst_ref=rows_of(buffer, me, chunk),
            send_sem=send_sem.at[index, chunk, target],
            recv_sem=recv_sem.at[index, chunk, slot],
            device_id={"seq": target},
            device_id_type=MESH,
        )

    def own_copy(index, chunk):
        source, buffer = inputs[index]
        return pltpu.make_async_copy(
            piece(source, me, groups, cols, chunk * width, width),
            rows_of(buffer, me, chunk),
            own_sem.at[index, chunk],
        )

    def returned(chunk, target, slot):
        return pltpu.make_async_remote_copy(
            src_ref=rows_of(ob, target, chunk),
            dst_ref=piece(o_ref, me, groups, cols, chunk * width, width),
            send_sem=back_send.at[chunk, target],
            recv_sem=back_recv.at[chunk, slot],
            device_id={"seq": target},
            device_id_type=MESH,
        )

    def own_return(chunk):
        return pltpu.make_async_copy(
            rows_of(ob, me, chunk),
            piece(o_ref, me, groups, cols, chunk * width, width),
            back_own.at[chunk],
        )

    ready = 1
    for chunk in range(chunks):
        if chunk == 0:
            line_start()
        elif ready < weight_steps:
            weight_step(ready)
            ready += 1
        for index in range(3):
            own_copy(index, chunk).start()

            @pl.loop(1, n)
            def _(step, index=index, chunk=chunk):
                outgoing(index, chunk, lax.rem(me + step, n), me).start()

    paired = 2 * head_width == LANES and width % LANES == 0
    unit = LANES if paired else head_width
    blocks = total_tokens // row_block

    for chunk in range(chunks):
        for index in range(3):
            own_copy(index, chunk).wait()

            @pl.loop(1, n)
            def _(step, index=index, chunk=chunk):
                other = lax.rem(me + step, n)
                outgoing(index, chunk, other, other).wait_recv()

        if paired:

            @pl.loop(0, (width // unit) * blocks)
            def _(step, chunk=chunk):
                attend_pair(
                    qb, kb, vb, ob,
                    pl.multiple_of((step % blocks) * row_block, row_block), row_block,
                    chunk * width + (step // blocks) * unit, head_width,
                )
        else:
            for head in range(width // unit):

                @pl.loop(0, blocks)
                def _(step, head=head, chunk=chunk):
                    attend_plain(
                        qb, kb, vb, ob,
                        pl.multiple_of(step * row_block, row_block), row_block,
                        chunk * width + head * unit, head_width,
                    )

        own_return(chunk).start()

        @pl.loop(1, n)
        def _(step, chunk=chunk):
            returned(chunk, lax.rem(me + step, n), me).start()

        if ready < weight_steps and chunk < chunks - 1:
            weight_step(ready)
            ready += 1

    for step in range(ready, weight_steps):
        weight_step(step)
    finish_weights()

    for chunk in range(chunks):
        own_return(chunk).wait()
        for index in range(3):

            @pl.loop(1, n)
            def _(step, index=index, chunk=chunk):
                outgoing(index, chunk, lax.rem(me + step, n), me).wait_send()

        @pl.loop(1, n)
        def _(step, chunk=chunk):
            other = lax.rem(me + step, n)
            returned(chunk, other, other).wait_recv()
            returned(chunk, other, me).wait_send()


def attention(queries, keys, values, embed_weight, up_weight):
    n = lax.axis_size("seq")
    group_count = lax.axis_size("groups")
    dom_count = lax.axis_size("dom")
    fan = 2 if n % 2 == 0 else 1
    particles, tokens, model_width = queries.shape
    head_width = model_width // HEADS
    per_device = particles * HEADS // n
    cols = per_device * head_width
    aligned = model_width % cols == 0 and cols % LANES == 0
    groups = model_width // cols if aligned else 0
    width = 2 * LANES if aligned and cols % (2 * LANES) == 0 else cols
    chunks = cols // width
    total_tokens = n * tokens

    def to_items(array):
        if aligned:
            return array
        split = array.reshape(particles, tokens, HEADS, head_width).transpose(0, 2, 1, 3)
        split = split.reshape(n, per_device, tokens, head_width).transpose(0, 2, 1, 3)
        return split.reshape(n, tokens, cols)

    operands = tuple(to_items(a) for a in (queries, keys, values))
    any_spec = pl.BlockSpec(memory_space=pl.ANY)
    embed_shape = (n * embed_weight.shape[0], embed_weight.shape[1])
    up_shape = (up_weight.shape[0], n * up_weight.shape[1])
    out, embed_full, up_full = pl.pallas_call(
        functools.partial(
            attention_kernel, n, fan, group_count, dom_count, groups, cols, width, head_width,
            min(256, total_tokens),
        ),
        out_shape=(
            jax.ShapeDtypeStruct(operands[0].shape, jnp.bfloat16),
            jax.ShapeDtypeStruct(embed_shape, jnp.bfloat16),
            jax.ShapeDtypeStruct(up_shape, jnp.bfloat16),
        ),
        in_specs=[any_spec] * 5,
        out_specs=(any_spec,) * 3,
        scratch_shapes=[pltpu.VMEM((total_tokens, cols), jnp.bfloat16)] * 4
        + [
            pltpu.SemaphoreType.DMA((3, chunks, n)),
            pltpu.SemaphoreType.DMA((3, chunks, n)),
            pltpu.SemaphoreType.DMA((3, chunks)),
            pltpu.SemaphoreType.DMA((chunks, n)),
            pltpu.SemaphoreType.DMA((chunks, n)),
            pltpu.SemaphoreType.DMA((chunks,)),
            pltpu.SemaphoreType.DMA((2,)),
            pltpu.SemaphoreType.DMA((2, 2, n // fan)),
            pltpu.SemaphoreType.DMA((2, 2, n // fan)),
            pltpu.SemaphoreType.DMA((2, fan, n // fan)),
            pltpu.SemaphoreType.DMA((2, fan, n // fan)),
            pltpu.SemaphoreType.DMA((2, group_count, n)),
            pltpu.SemaphoreType.DMA((2, group_count, n)),
            pltpu.SemaphoreType.DMA((2, dom_count, group_count, n)),
            pltpu.SemaphoreType.DMA((2, dom_count, group_count, n)),
        ],
        compiler_params=pltpu.CompilerParams(
            collective_id=0, has_side_effects=True, vmem_limit_bytes=60 * 1024 * 1024
        ),
        name="attention",
    )(*operands, embed_weight, up_weight)
    if not aligned:
        out = out.reshape(n, tokens, per_device, head_width).transpose(0, 2, 1, 3)
        out = out.reshape(particles, HEADS, tokens, head_width).transpose(0, 2, 1, 3)
    return out.reshape(particles * tokens, model_width), embed_full, up_full


def reward_kernel(n, doms, particles, x_ref, o_ref, held, send_sem, recv_sem):
    me = lax.axis_index("dom") * n + lax.axis_index("seq")
    members = n * doms

    def target(step):
        other = lax.rem(me + step, members)
        return other, {"dom": other // n, "seq": other % n}

    def copy(step, slot):
        other, device = target(step)
        return pltpu.make_async_remote_copy(
            src_ref=x_ref,
            dst_ref=held.at[me],
            send_sem=send_sem.at[other],
            recv_sem=recv_sem.at[slot],
            device_id=device,
            device_id_type=MESH,
        )

    barrier = pltpu.get_barrier_semaphore()

    @pl.loop(1, members)
    def _(step):
        _, device = target(step)
        pl.semaphore_signal(barrier, inc=1, device_id=device, device_id_type=MESH)

    pl.semaphore_wait(barrier, members - 1)

    @pl.loop(1, members)
    def _(step):
        copy(step, me).start()

    held[me] = x_ref[...]

    @pl.loop(1, members)
    def _(step):
        copy(step, lax.rem(me + step, members)).wait_recv()

    logits = []
    for dom in range(doms):
        rewards = jnp.sum(held[dom * n : (dom + 1) * n], axis=0)[:1]
        value = held[dom * n][1:2] + potential_scale * rewards
        used = lax.broadcasted_iota(jnp.int32, value.shape, 1) < particles
        logits.append(jnp.where(used, value, -jnp.inf))
    highest = functools.reduce(jnp.maximum, [jnp.max(v, axis=1, keepdims=True) for v in logits])
    total = sum(jnp.sum(jnp.exp(v - highest), axis=1, keepdims=True) for v in logits)
    own = logits[0]
    for dom in range(1, doms):
        own = jnp.where(lax.axis_index("dom") == dom, logits[dom], own)
    o_ref[...] = jnp.broadcast_to(own - (highest + jnp.log(total)), o_ref.shape)

    @pl.loop(1, members)
    def _(step):
        copy(step, me).wait_send()


def weigh(partial_value, prev_logw, n, doms):
    particles = partial_value.shape[0]
    rows = jnp.stack([partial_value, prev_logw])
    padded = jnp.pad(rows, ((0, 8 - 2), (0, LANES - particles)))
    vmem = pl.BlockSpec(memory_space=pltpu.VMEM)
    out = pl.pallas_call(
        functools.partial(reward_kernel, n, doms, particles),
        out_shape=jax.ShapeDtypeStruct((8, LANES), jnp.float32),
        in_specs=[vmem],
        out_specs=vmem,
        scratch_shapes=[
            pltpu.VMEM((n * doms, 8, LANES), jnp.float32),
            pltpu.SemaphoreType.DMA((n * doms,)),
            pltpu.SemaphoreType.DMA((n * doms,)),
        ],
        compiler_params=pltpu.CompilerParams(collective_id=1, has_side_effects=True),
        name="rewards",
    )(padded)
    return out[0, :particles]


def on_device(
    latents,
    queries,
    keys,
    values,
    out_weight,
    step_index,
    embed_weight,
    norm_gain,
    up_weight,
    head_weight,
    prev_logw,
    ancestors,
):
    seq_count = lax.axis_size("seq")
    dom_count = lax.axis_size("dom")
    local_particles, local_tokens, model_width = latents.shape
    local_rows = local_particles * local_tokens
    total_tokens = local_tokens * seq_count
    dom = lax.axis_index("dom")

    attended, embed_full, up_full = attention(
        queries, keys, values, embed_weight, up_weight
    )
    flat = latents.reshape(local_rows, model_width).astype(jnp.float32)
    velocity = flat + jnp.dot(attended, out_weight, preferred_element_type=jnp.float32)
    sigma = step_index[0].astype(jnp.float32) / STEPS
    clean = (flat - sigma * velocity).astype(jnp.bfloat16)
    stepped = (flat - velocity / STEPS).astype(jnp.bfloat16)
    stepped = stepped.reshape(local_particles, local_tokens, model_width)
    candidates = [stepped]
    for shift in range(1, dom_count):
        pairs = [((to + shift) % dom_count, to) for to in range(dom_count)]
        candidates.append(lax.ppermute(stepped, "dom", pairs))
    embedded = jnp.dot(
        clean,
        embed_full,
        preferred_element_type=jnp.float32,
    )
    centre = jnp.mean(embedded, axis=1, keepdims=True)
    centered = embedded - centre
    variance = jnp.mean(centered * centered, axis=1, keepdims=True)
    features = jax.nn.gelu(centered * lax.rsqrt(variance + norm_eps) * norm_gain[None, :]).astype(
        jnp.bfloat16
    )
    scored = (
        jax.nn.gelu(
            jnp.dot(
                features,
                up_full,
                preferred_element_type=jnp.float32,
            )
        )
        * head_weight[None, :]
    )
    partial_value = jnp.sum(jnp.sum(scored, axis=1).reshape(local_particles, local_tokens), axis=1)
    partial_value = partial_value / math.sqrt(total_tokens)
    log_weights = weigh(partial_value, prev_logw, seq_count, dom_count)
    slot = lax.rem(ancestors // local_particles - dom + dom_count, dom_count)
    row = slot * local_particles + lax.rem(ancestors, local_particles)
    resampled = jnp.take(jnp.concatenate(candidates), row, axis=0, mode="clip")
    return (resampled, log_weights)


def solution(mesh):
    in_specs = (
        P(("groups", "dom"), "seq", None),
        P(("groups", "dom"), "seq", None),
        P(("groups", "dom"), "seq", None),
        P(("groups", "dom"), "seq", None),
        P(),
        P("groups"),
        P("seq", None),
        P(),
        P(None, "seq"),
        P(),
        P(("groups", "dom")),
        P(("groups", "dom")),
    )
    out_specs = (P(("groups", "dom"), "seq", None), P(("groups", "dom")))
    return jax.shard_map(
        on_device, mesh=mesh, in_specs=in_specs, out_specs=out_specs, check_vma=False
    )
```

profile of v0, /device:TPU:0, one launch (start us, length us, event | category | flops | bytes accessed | tf_op | source)
XLA Modules:
  0.0 126.9 jit_solution(5292684310287864175)
XLA Ops:
  0.6 100.4 %attention.1 = (bf16[4,64,1536]{2,1,0:T(8,128)(2,1)}, bf16[1536,1024]{1,0:T(8,128)(2,1)}, bf16[1024,4096]{1,0:T(8,128)(2,1)}) custom-call(bf16[4,64,1536]{2,1,0:T(8,128)(2,1)} %q_ref.1, bf16[4,64,1536]{2,1,0:T(8,128)(2,1)} %k_ref.1, bf16[4,64,1536]{2,1,0:T(8,128)(2,1)} %v_ref.1, bf16[192,1024]{1,0:T(8,128)(2,1)} %embed_ref.1, bf16[1024,512]{1,0:T(8,128)(2,1)} %up_ref.1), custom_call_target="tpu_custom_call" | custom-call | tf_op jit(solution)/shard_map/attention/pallas_call | solution.py:450
  101.0 0.0 copy-start
  101.0 0.0 copy-start.1
  101.0 0.0 copy-start.3
  101.0 4.6 %fusion.9 = (bf16[256,1536]{1,0:T(8,128)(2,1)S(1)}, f32[256,1536]{1,0:T(8,128)S(1)}) fusion(bf16[4,64,1536]{2,1,0:T(8,128)(2,1)} %param.12, bf16[256,1536]{1,0:T(8,128)(2,1)} %bitcast.20, bf16[1536,1536]{1,0:T(8,128)(2,1)} %param.16, bf16[256,1536]{1,0:T(8,128)(2,1)} %bitcast.17), kind=kOutput, calls=%fused_computation.14 | convolution fusion | flops 1210318848 | bytes 9437184 | tf_op jit(solution)/shard_map/dot_general | solution.py:593
  105.7 0.0 copy-start.4
  105.7 0.0 copy-start.5
  105.7 0.1 collective-permute-start
  107.3 0.0 copy-done
  107.3 0.0 copy-done.1
  107.3 1.1 fusion.40
  108.4 0.3 multiply_reduce_fusion
  108.6 0.0 copy-done.3
  108.6 0.0 copy-done.4
  108.6 0.0 copy-done.5
  108.7 0.0 copy-start.2
  108.7 0.0 copy-start.6
  108.7 4.3 %fusion.8 = f32[256]{0:T(256)S(1)} fusion(f32[4096]{0:T(1024)S(1)} %copy-done.4, bf16[1024,4096]{1,0:T(8,128)(2,1)S(1)} %copy-done.3, f32[256,1024]{1,0:T(8,128)S(1)} %get-tuple-element.11, f32[1024]{0:T(1024)S(1)} %copy-done.5, f32[256]{0:T(256)S(1)} %add_rsqrt_fusion, f32[256]{0:T(256)S(1)} %broadcast_multiply_fusion), kind=kOutput, calls=%fused_computation.10 | convolution fusion | flops 2161114880 | bytes 9460736 | tf_op jit(solution)/shard_map/dot_general | solution.py:615
  113.0 0.1 reshape.44
  113.1 0.1 reduce_sum.39
  113.2 0.0 copy-done.2
  113.2 0.6 select_maximum_fusion.x_ref
  113.8 10.2 %rewards.1 = f32[8,128]{1,0:T(8,128)} custom-call(f32[8,128]{1,0:T(8,128)} %select_maximum_fusion.x_ref), custom_call_target="tpu_custom_call" | custom-call | tf_op jit(solution)/shard_map/rewards/pallas_call | solution.py:552
  124.0 0.0 copy-done.6
  124.1 1.2 slice_bitcast_fusion
  125.3 0.0 collective-permute-done
  125.3 0.1 pad_maximum_fusion
  125.4 1.5 %gather_fusion = bf16[4,64,1536]{2,1,0:T(8,128)(2,1)} fusion(bf16[8,64,1536]{2,1,0:T(8,128)(2,1)S(1)} %pad_maximum_fusion, s32[1024]{0:T(1024)S(1)} %pad_clamp_fusion), kind=kCustom, calls=%fused_computation | custom fusion | bytes 1572880 | tf_op jit(solution)/shard_map/jit(_take)/gather | solution.py:628
  (5 shorter events, 0.0 us)
Async XLA Ops:
  101.0 6.2 %copy-start = (bf16[1536,1024]{1,0:T(8,128)(2,1)S(1)}, bf16[1536,1024]{1,0:T(8,128)(2,1)}, u32[]{:S(2)}) copy-start(bf16[1536,1024]{1,0:T(8,128)(2,1)} %get-tuple-element.6) | copy-start | bytes 9437188
  101.0 6.2 %copy-start.1 = (bf16[4,64,1536]{2,1,0:T(8,128)(2,1)S(1)}, bf16[4,64,1536]{2,1,0:T(8,128)(2,1)}, u32[]{:S(2)}) copy-start(bf16[4,64,1536]{2,1,0:T(8,128)(2,1)} %param.12) | copy-start | bytes 2359300
  101.0 7.6 %copy-start.3 = (bf16[1024,4096]{1,0:T(8,128)(2,1)S(1)}, bf16[1024,4096]{1,0:T(8,128)(2,1)}, u32[]{:S(2)}) copy-start(bf16[1024,4096]{1,0:T(8,128)(2,1)} %get-tuple-element.7) | copy-start | bytes 25165828
  105.7 2.9 %copy-start.4 = (f32[4096]{0:T(1024)S(1)}, f32[4096]{0:T(1024)}, u32[]{:S(2)}) copy-start(f32[4096]{0:T(1024)} %param.21) | copy-start | bytes 49156
  105.7 2.9 %copy-start.5 = (f32[1024]{0:T(1024)S(1)}, f32[1024]{0:T(1024)}, u32[]{:S(2)}) copy-start(f32[1024]{0:T(1024)} %param.19) | copy-start | bytes 12292
  105.7 19.6 %collective-permute-start = (bf16[4,64,1536]{2,1,0:T(8,128)(2,1)S(1)}, bf16[4,64,1536]{2,1,0:T(8,128)(2,1)S(1)}, u32[]{:S(2)}, u32[]{:S(2)}) collective-permute-start(bf16[4,64,1536]{2,1,0:T(8,128)(2,1)S(1)} %bitcast.15), channel_id=1, source_target_pairs={{8,0},{0,8},{9,1},{1,9},{10,2},{2,10},{11,3},{3,11},{12,4},{4,12},... | collective-permute-start | bytes 2359304 | tf_op jit(solution)/shard_map/ppermute | solution.py:601
  108.7 4.6 %copy-start.2 = (f32[4]{0:T(128)S(1)}, f32[4]{0:T(128)}, u32[]{:S(2)}) copy-start(f32[4]{0:T(128)} %param.22) | copy-start | bytes 52
  108.7 15.4 %copy-start.6 = (s32[4]{0:T(128)S(1)}, s32[4]{0:T(128)}, u32[]{:S(2)}) copy-start(s32[4]{0:T(128)} %param.23) | copy-start | bytes 52
where the time goes:
time: 127 us
  Pallas kernels  111 us (87%)
  matrix products  10.1 us (8%)
  local copies, waits for them, and re-layouts  2.79 us (2%)
  between operations  2.27 us (2%)
    pallas_call x1, Pallas kernels, attention(): pl.pallas_call(functools.partial(attention_kernel, n, fan, group_count, d...  100 us
    pallas_call x1, Pallas kernels, weigh(): pl.pallas_call(functools.partial(reward_kernel, n, doms, particles), out_...  10.2 us
    dot_general x1, matrix products, on_device(): jnp.dot(attended, out_weight, preferred_element_type=jnp.float32)  4.64 us
    dot_general x1, matrix products, on_device(): jnp.dot(features, up_full, preferred_element_type=jnp.float32)  4.33 us
  transfers between devices with their start and end apart: 1, of which 0 were waited for; matrix products, arithmetic and copies ran while one was open for 6% of the time, Pallas kernels for 8%

commit v1 on v0

--- a/solution.py
+++ b/solution.py
@@ -76,37 +76,14 @@
     return ref.at[item // groups, :, pl.ds(offset, width)]
 
 
-def attention_kernel(
-    n, fan, group_count, dom_count, groups, cols, width, head_width, row_block,
-    q_ref, k_ref, v_ref, embed_ref, up_ref, o_ref, embed_full, up_full,
-    qb, kb, vb, ob, send_sem, recv_sem, own_sem, back_send, back_recv, back_own,
+def weight_exchange(
+    n, fan, group_count, dom_count, embed_ref, up_ref, embed_full, up_full,
     shard_own, line_send, line_recv, fan_send, fan_recv, group_send, group_recv, dom_send, dom_recv,
 ):
     me = lax.axis_index("seq")
     my_group = lax.axis_index("groups")
     my_dom = lax.axis_index("dom")
     share_count = group_count * dom_count
-    tokens = q_ref.shape[1]
-    total_tokens = n * tokens
-    chunks = cols // width
-    inputs = ((q_ref, qb), (k_ref, kb), (v_ref, vb))
-
-    barrier = pltpu.get_barrier_semaphore()
-
-    @pl.loop(1, n)
-    def _(step):
-        pl.semaphore_signal(
-            barrier, inc=1, device_id={"seq": lax.rem(me + step, n)}, device_id_type=MESH
-        )
-
-    for step in range(1, group_count):
-        peer = {"groups": lax.rem(my_group + step, group_count)}
-        pl.semaphore_signal(barrier, inc=1, device_id=peer, device_id_type=MESH)
-    for step in range(1, dom_count):
-        peer = {"dom": lax.rem(my_dom + step, dom_count)}
-        pl.semaphore_signal(barrier, inc=1, device_id=peer, device_id_type=MESH)
-    pl.semaphore_wait(barrier, n - 1 + group_count - 1 + dom_count - 1)
-
     embed_rows, embed_cols = embed_ref.shape
     up_rows, up_cols = up_ref.shape
     embed_part = embed_cols // share_count
@@ -280,8 +257,8 @@
 
     weight_steps = length + 2
 
-    def finish_weights():
-        for which in range(2):
+    def finish_weights(parts=(0, 1)):
+        for which in parts:
             shard_copy(which).wait()
             for direction in range(2):
                 for step in range(1, length):
@@ -304,6 +281,45 @@
                     for group_shift in range(group_count):
                         dom_copy(which, owner, shift, group_shift, True).wait_recv()
                         dom_copy(which, owner, shift, group_shift, False).wait_send()
+
+    return line_start, weight_step, finish_weights, weight_steps
+
+
+def attention_kernel(
+    n, fan, group_count, dom_count, groups, cols, width, head_width, row_block,
+    q_ref, k_ref, v_ref, embed_ref, up_ref, o_ref, embed_full, up_full,
+    qb, kb, vb, ob, send_sem, recv_sem, own_sem, back_send, back_recv, back_own,
+    shard_own, line_send, line_recv, fan_send, fan_recv, group_send, group_recv, dom_send, dom_recv,
+):
+    me = lax.axis_index("seq")
+    my_group = lax.axis_index("groups")
+    my_dom = lax.axis_index("dom")
+    tokens = q_ref.shape[1]
+    total_tokens = n * tokens
+    chunks = cols // width
+    inputs = ((q_ref, qb), (k_ref, kb), (v_ref, vb))
+
+    barrier = pltpu.get_barrier_semaphore()
+
+    @pl.loop(1, n)
+    def _(step):
+        pl.semaphore_signal(
+            barrier, inc=1, device_id={"seq": lax.rem(me + step, n)}, device_id_type=MESH
+        )
+
+    for step in range(1, group_count):
+        peer = {"groups": lax.rem(my_group + step, group_count)}
+        pl.semaphore_signal(barrier, inc=1, device_id=peer, device_id_type=MESH)
+    for step in range(1, dom_count):
+        peer = {"dom": lax.rem(my_dom + step, dom_count)}
+        pl.semaphore_signal(barrier, inc=1, device_id=peer, device_id_type=MESH)
+    pl.semaphore_wait(barrier, n - 1 + group_count - 1 + dom_count - 1)
+
+    line_start, weight_step, finish_weights, weight_steps = weight_exchange(
+        n, fan, group_count, dom_count, embed_ref, up_ref, embed_full, up_full,
+        shard_own, line_send, line_recv, fan_send, fan_recv, group_send, group_recv,
+        dom_send, dom_recv,
+    )
 
     def rows_of(ref, owner, chunk):
         row = pl.ds(pl.multiple_of(owner * tokens, 16), tokens)
@@ -565,6 +581,408 @@
     return out[0, :particles]
 
 
+def part_sum(block, rows):
+    parts = [
+        jnp.sum(block[at : at + rows], axis=0, keepdims=True)
+        for at in range(0, block.shape[0], rows)
+    ]
+    return jnp.concatenate(parts, axis=0)
+
+
+def fused_kernel(
+    n, fan, group_count, dom_count, groups, chunks, head_width, row_block, tile,
+    q_ref, k_ref, v_ref, lat_ref, wo_ref, step_ref, embed_ref, gain_ref, up_ref, head_ref,
+    prev_ref, anc_ref, out_ref, logw_ref,
+    qb, kb, vb, ob, mixed, embed_full, up_full, wo, lat, velocity, clean, embedded, features,
+    cand, score, mine, held,
+    send_sem, recv_sem, own_sem, back_send, back_recv, back_own,
+    shard_own, line_send, line_recv, fan_send, fan_recv, group_send, group_recv, dom_send, dom_recv,
+    load_sem, step_send, step_recv, score_send, score_recv,
+):
+    me = lax.axis_index("seq")
+    my_group = lax.axis_index("groups")
+    my_dom = lax.axis_index("dom")
+    particles, tokens, model_width = q_ref.shape
+    rows = particles * tokens
+    cols = model_width // groups
+    total_tokens = n * tokens
+    inputs = ((q_ref, qb), (k_ref, kb), (v_ref, vb))
+    members = n * dom_count
+    member = my_dom * n + me
+
+    def other_member(step):
+        other = lax.rem(member + step, members)
+        return other, {"dom": other // n, "seq": other % n}
+
+    loads = (
+        pltpu.make_async_copy(wo_ref, wo, load_sem.at[0]),
+        pltpu.make_async_copy(lat_ref, lat, load_sem.at[1]),
+    )
+
+    barrier = pltpu.get_barrier_semaphore()
+
+    @pl.loop(1, members)
+    def _(step):
+        _, device = other_member(step)
+        pl.semaphore_signal(barrier, inc=1, device_id=device, device_id_type=MESH)
+
+    for step in range(1, group_count):
+        peer = {"groups": lax.rem(my_group + step, group_count)}
+        pl.semaphore_signal(barrier, inc=1, device_id=peer, device_id_type=MESH)
+    for load in loads:
+        load.start()
+    pl.semaphore_wait(barrier, members - 1 + group_count - 1)
+
+    line_start, weight_step, finish_weights, weight_steps = weight_exchange(
+        n, fan, group_count, dom_count, embed_ref, up_ref, embed_full, up_full,
+        shard_own, line_send, line_recv, fan_send, fan_recv, group_send, group_recv,
+        dom_send, dom_recv,
+    )
+
+    def source_of(ref, item, chunk):
+        start, width = chunks[chunk]
+        offset = pl.multiple_of(groups * start + (item % groups) * width, LANES)
+        return ref.at[item // groups, :, pl.ds(offset, width)]
+
+    def mixed_of(item, chunk):
+        start, width = chunks[chunk]
+        offset = pl.multiple_of(groups * start + (item % groups) * width, LANES)
+        row = pl.multiple_of((item // groups) * tokens, 16)
+        return mixed.at[pl.ds(row, tokens), pl.ds(offset, width)]
+
+    def rows_of(ref, owner, chunk):
+        start, width = chunks[chunk]
+        row = pl.ds(pl.multiple_of(owner * tokens, 16), tokens)
+        return ref.at[row, pl.ds(start, width)]
+
+    def outgoing(index, chunk, target, slot):
+        source, buffer = inputs[index]
+        return pltpu.make_async_remote_copy(
+            src_ref=source_of(source, target, chunk),
+            dst_ref=rows_of(buffer, me, chunk),
+            send_sem=send_sem.at[index, chunk, target],
+            recv_sem=recv_sem.at[index, chunk, slot],
+            device_id={"seq": target},
+            device_id_type=MESH,
+        )
+
+    def own_copy(index, chunk):
+        source, buffer = inputs[index]
+        return pltpu.make_async_copy(
+            source_of(source, me, chunk), rows_of(buffer, me, chunk), own_sem.at[index, chunk]
+        )
+
+    def returned(chunk, target, slot):
+        return pltpu.make_async_remote_copy(
+            src_ref=rows_of(ob, target, chunk),
+            dst_ref=mixed_of(me, chunk),
+            send_sem=back_send.at[chunk, target],
+            recv_sem=back_recv.at[chunk, slot],
+            device_id={"seq": target},
+            device_id_type=MESH,
+        )
+
+    def own_return(chunk):
+        return pltpu.make_async_copy(
+            rows_of(ob, me, chunk), mixed_of(me, chunk), back_own.at[chunk]
+        )
+
+    count = len(chunks)
+    ready = 1
+    for chunk in range(count):
+        if chunk == 0:
+            line_start()
+        elif ready < weight_steps:
+            weight_step(ready)
+            ready += 1
+        for index in range(3):
+            own_copy(index, chunk).start()
+
+            @pl.loop(1, n)
+            def _(step, index=index, chunk=chunk):
+                outgoing(index, chunk, lax.rem(me + step, n), me).start()
+
+    blocks = total_tokens // row_block
+
+    for chunk in range(count):
+        start, width = chunks[chunk]
+        for index in range(3):
+            own_copy(index, chunk).wait()
+
+            @pl.loop(1, n)
+            def _(step, index=index, chunk=chunk):
+                other = lax.rem(me + step, n)
+                outgoing(index, chunk, other, other).wait_recv()
+
+        @pl.loop(0, (width // LANES) * blocks)
+        def _(step, start=start):
+            attend_pair(
+                qb, kb, vb, ob,
+                pl.multiple_of((step % blocks) * row_block, row_block), row_block,
+                start + (step // blocks) * LANES, head_width,
+            )
+
+        own_return(chunk).start()
+
+        @pl.loop(1, n)
+        def _(step, chunk=chunk):
+            returned(chunk, lax.rem(me + step, n), me).start()
+
+        if ready < weight_steps and chunk < count - 1:
+            weight_step(ready)
+            ready += 1
+
+    for step in range(ready, weight_steps):
+        weight_step(step)
+    for load in loads:
+        load.wait()
+
+    sigma = step_ref[0].astype(jnp.float32) / STEPS
+
+    for chunk in range(count):
+        start, width = chunks[chunk]
+        inner = pl.ds(groups * start, groups * width)
+        own_return(chunk).wait()
+
+        @pl.loop(1, n)
+        def _(step, chunk=chunk):
+            other = lax.rem(me + step, n)
+            returned(chunk, other, other).wait_recv()
+
+        @pl.loop(0, model_width // tile)
+        def _(step, chunk=chunk, inner=inner):
+            columns = pl.ds(pl.multiple_of(step * tile, tile), tile)
+            part = jnp.dot(mixed[:, inner], wo[inner, columns], preferred_element_type=jnp.float32)
+            if chunk > 0:
+                part = velocity[:, columns] + part
+            if chunk < count - 1:
+                velocity[:, columns] = part
+                return
+            flat = lat[:, :, columns].reshape(rows, tile).astype(jnp.float32)
+            moved = flat + part
+            clean[:, columns] = (flat - sigma * moved).astype(jnp.bfloat16)
+            stepped = (flat - moved / STEPS).astype(jnp.bfloat16)
+            for item in range(particles):
+                cand[my_dom * particles + item, :, columns] = stepped[
+                    item * tokens : (item + 1) * tokens
+                ]
+
+    finish_weights((0,))
+
+    @pl.loop(0, embedded.shape[1] // tile)
+    def _(step):
+        columns = pl.ds(pl.multiple_of(step * tile, tile), tile)
+        embedded[:, columns] = jnp.dot(
+            clean[...], embed_full[:, columns], preferred_element_type=jnp.float32
+        )
+
+    def step_copy(shift, incoming):
+        source = lax.rem(my_dom - shift + dom_count, dom_count) if incoming else my_dom
+        block = cand.at[pl.ds(source * particles, particles)]
+        return pltpu.make_async_remote_copy(
+            src_ref=block,
+            dst_ref=block,
+            send_sem=step_send.at[shift],
+            recv_sem=step_recv.at[shift],
+            device_id={"dom": lax.rem(my_dom + shift, dom_count)},
+            device_id_type=MESH,
+        )
+
+    for shift in range(1, dom_count):
+        step_copy(shift, False).start()
+
+    @pl.loop(0, particles)
+    def _(item):
+        own_rows = pl.ds(pl.multiple_of(item * tokens, tokens), tokens)
+        block = embedded[own_rows, :]
+        centered = block - jnp.mean(block, axis=1, keepdims=True)
+        variance = jnp.mean(centered * centered, axis=1, keepdims=True)
+        normed = centered * lax.rsqrt(variance + norm_eps) * gain_ref[...]
+        features[own_rows, :] = jax.nn.gelu(normed).astype(jnp.bfloat16)
+
+    finish_weights((1,))
+    score[...] = jnp.zeros_like(score)
+
+    @pl.loop(0, up_full.shape[1] // tile)
+    def _(step):
+        columns = pl.ds(pl.multiple_of(step * tile, tile), tile)
+        hidden = jnp.dot(features[...], up_full[:, columns], preferred_element_type=jnp.float32)
+        score[...] += part_sum(jax.nn.gelu(hidden), tokens) * head_ref[:, columns]
+
+    partial_value = jnp.sum(score[...], axis=1, keepdims=True) / math.sqrt(total_tokens)
+    lane = lax.broadcasted_iota(jnp.int32, (particles, LANES), 1)
+    row = lax.broadcasted_iota(jnp.int32, (particles, LANES), 0)
+    before = jnp.zeros((particles, LANES), jnp.float32)
+    for item in range(particles):
+        before = jnp.where(row == item, prev_ref[item], before)
+    half = LANES // 2
+    own_block = jnp.where(lane < half, partial_value, before)
+    mine[0:particles, :] = own_block
+    held[member, 0:particles, :] = own_block
+
+    def score_copy(step, slot):
+        other, device = other_member(step)
+        return pltpu.make_async_remote_copy(
+            src_ref=mine,
+            dst_ref=held.at[member],
+            send_sem=score_send.at[other],
+            recv_sem=score_recv.at[slot],
+            device_id=device,
+            device_id_type=MESH,
+        )
+
+    @pl.loop(1, members)
+    def _(step):
+        score_copy(step, member).start()
+
+    for shift in range(1, dom_count):
+        step_copy(shift, True).wait_recv()
+    for item in range(particles):
+        out_ref[item] = cand[anc_ref[item]]
+
+    for chunk in range(count):
+        for index in range(3):
+
+            @pl.loop(1, n)
+            def _(step, index=index, chunk=chunk):
+                outgoing(index, chunk, lax.rem(me + step, n), me).wait_send()
+
+        @pl.loop(1, n)
+        def _(step, chunk=chunk):
+            returned(chunk, lax.rem(me + step, n), me).wait_send()
+
+    for shift in range(1, dom_count):
+        step_copy(shift, False).wait_send()
+
+    @pl.loop(1, members)
+    def _(step):
+        score_copy(step, lax.rem(member + step, members)).wait_recv()
+
+    logits = []
+    for dom in range(dom_count):
+        reward = jnp.sum(held[dom * n : (dom + 1) * n, 0:particles, :], axis=0)[:, 0:1]
+        logits.append(held[dom * n, 0:particles, :][:, half : half + 1] + potential_scale * reward)
+    highest = functools.reduce(
+        jnp.maximum, [jnp.max(value, axis=0, keepdims=True) for value in logits]
+    )
+    total = sum(jnp.sum(jnp.exp(value - highest), axis=0, keepdims=True) for value in logits)
+    own = logits[0]
+    for dom in range(1, dom_count):
+        own = jnp.where(my_dom == dom, logits[dom], own)
+    logw_ref[0:particles, :] = jnp.broadcast_to(
+        own - (highest + jnp.log(total)), (particles, LANES)
+    )
+
+    @pl.loop(1, members)
+    def _(step):
+        score_copy(step, member).wait_send()
+
+
+def chunk_widths(cols):
+    widths = []
+    left = cols
+    while left > 2 * LANES + LANES:
+        widths.append(2 * LANES)
+        left -= 2 * LANES
+    widths += [LANES] * (left // LANES)
+    starts = [sum(widths[:i]) for i in range(len(widths))]
+    return tuple(zip(starts, widths))
+
+
+def fused(
+    latents, queries, keys, values, out_weight, step_index, embed_weight, norm_gain, up_weight,
+    head_weight, prev_logw, ancestors,
+):
+    n = lax.axis_size("seq")
+    group_count = lax.axis_size("groups")
+    dom_count = lax.axis_size("dom")
+    fan = 2 if n % 2 == 0 else 1
+    particles, tokens, model_width = queries.shape
+    head_width = model_width // HEADS
+    cols = particles * model_width // n
+    groups = model_width // cols
+    chunks = chunk_widths(cols)
+    count = len(chunks)
+    rows = particles * tokens
+    total_tokens = n * tokens
+    members = n * dom_count
+    tile = 512
+    embed_shape = (n * embed_weight.shape[0], embed_weight.shape[1])
+    up_shape = (up_weight.shape[0], n * up_weight.shape[1])
+    hbm = pl.BlockSpec(memory_space=pl.ANY)
+    vmem = pl.BlockSpec(memory_space=pltpu.VMEM)
+    smem = pl.BlockSpec(memory_space=pltpu.SMEM)
+    bf16 = jnp.bfloat16
+    dma = pltpu.SemaphoreType.DMA
+    resampled, logw = pl.pallas_call(
+        functools.partial(
+            fused_kernel, n, fan, group_count, dom_count, groups, chunks, head_width,
+            min(256, total_tokens), tile,
+        ),
+        out_shape=(
+            jax.ShapeDtypeStruct(latents.shape, bf16),
+            jax.ShapeDtypeStruct((8, LANES), jnp.float32),
+        ),
+        in_specs=[hbm] * 5 + [smem, hbm, vmem, hbm, vmem, smem, smem],
+        out_specs=(vmem, vmem),
+        scratch_shapes=[pltpu.VMEM((total_tokens, cols), bf16)] * 4
+        + [
+            pltpu.VMEM((rows, model_width), bf16),
+            pltpu.VMEM(embed_shape, bf16),
+            pltpu.VMEM(up_shape, bf16),
+            pltpu.VMEM(out_weight.shape, bf16),
+            pltpu.VMEM(latents.shape, bf16),
+            pltpu.VMEM((rows, model_width), jnp.float32),
+            pltpu.VMEM((rows, model_width), bf16),
+            pltpu.VMEM((rows, embed_shape[1]), jnp.float32),
+            pltpu.VMEM((rows, embed_shape[1]), bf16),
+            pltpu.VMEM((dom_count * particles, tokens, model_width), bf16),
+            pltpu.VMEM((particles, tile), jnp.float32),
+            pltpu.VMEM((8, LANES), jnp.float32),
+            pltpu.VMEM((members, 8, LANES), jnp.float32),
+            dma((3, count, n)),
+            dma((3, count, n)),
+            dma((3, count)),
+            dma((count, n)),
+            dma((count, n)),
+            dma((count,)),
+            dma((2,)),
+            dma((2, 2, n // fan)),
+            dma((2, 2, n // fan)),
+            dma((2, fan, n // fan)),
+            dma((2, fan, n // fan)),
+            dma((2, group_count, n)),
+            dma((2, group_count, n)),
+            dma((2, dom_count, group_count, n)),
+            dma((2, dom_count, group_count, n)),
+            dma((2,)),
+            dma((dom_count,)),
+            dma((dom_count,)),
+            dma((members,)),
+            dma((members,)),
+        ],
+        compiler_params=pltpu.CompilerParams(
+            collective_id=0, has_side_effects=True, vmem_limit_bytes=60 * 1024 * 1024
+        ),
+        name="step",
+    )(
+        queries, keys, values, latents, out_weight, step_index, embed_weight,
+        norm_gain.reshape(1, -1), up_weight, head_weight.reshape(1, -1), prev_logw, ancestors,
+    )
+    return resampled, logw[:particles, 0]
+
+
+def tiles_evenly(queries, embed_weight, up_weight):
+    n = lax.axis_size("seq")
+    particles, tokens, model_width = queries.shape
+    if particles * HEADS % n:
+        return False
+    cols = particles * model_width // n
+    if 2 * (model_width // HEADS) != LANES or cols % LANES or model_width % cols:
+        return False
+    return model_width % 512 == 0 and embed_weight.shape[1] % 512 == 0
+
+
 def on_device(
     latents,
     queries,
@@ -586,6 +1004,11 @@
     total_tokens = local_tokens * seq_count
     dom = lax.axis_index("dom")
 
+    if tiles_evenly(queries, embed_weight, up_weight):
+        return fused(
+            latents, queries, keys, values, out_weight, step_index, embed_weight, norm_gain,
+            up_weight, head_weight, prev_logw, ancestors,
+        )
     attended, embed_full, up_full = attention(
         queries, keys, values, embed_weight, up_weight
     )

time: 127 us -> 122 us (0.961)
  matrix products: 10.1 us -> 0 us
  Pallas kernels: 111 us -> 117 us
    dot_general x3 -> x0, matrix products: 10.1 us -> none  [the longest x1 4.64 us: on_device(): jnp.dot(attended, out_weight, preferred_element_type=jnp.float32)]
    pallas_call x2 -> x1, Pallas kernels: 111 us -> 117 us  [fused(): pl.pallas_call(functools.partial(fused_kernel, n, fan, group_count, dom_c...]
    unnamed x14 -> x1, local copies, waits for them, and re-layouts: 0.04 us -> 2.06 us
    gather x1 -> x0, local copies, waits for them, and re-layouts: 1.48 us -> none  [on_device(): resampled = jnp.take(jnp.concatenate(candidates), row, axis=0, mode='clip')]
    slice x0 -> x1, local copies, waits for them, and re-layouts: none -> 1.3 us  [fused(): return (resampled, logw[:particles, 0])]
  transfers between devices with their start and end apart: 1 -> 0, of which waited for: 0 -> 0; matrix products, arithmetic and copies ran while one was open for 6% -> 0% of each run, Pallas kernels for 8% -> 0%
where the time goes in v1:
time: 122 us
  Pallas kernels  117 us (96%)
  local copies, waits for them, and re-layouts  3.36 us (3%)
  between operations  1.29 us (1%)
    pallas_call x1, Pallas kernels, fused(): pl.pallas_call(functools.partial(fused_kernel, n, fan, group_count, dom_c...  117 us

profile of v1, /device:TPU:0, one launch (start us, length us, event | category | flops | bytes accessed | tf_op | source)
XLA Modules:
  0.0 121.6 jit_solution(14222531392691171616)
XLA Ops:
  1.3 116.9 %step.1 = (bf16[4,64,1536]{2,1,0:T(8,128)(2,1)}, f32[8,128]{1,0:T(8,128)}) custom-call(bf16[4,64,1536]{2,1,0:T(8,128)(2,1)} %q_ref.1, bf16[4,64,1536]{2,1,0:T(8,128)(2,1)} %k_ref.1, bf16[4,64,1536]{2,1,0:T(8,128)(2,1)} %v_ref.1, bf16[4,64,1536]{2,1,0:T(8,128)(2,1)} %lat_ref.1, bf16[1536,1536]{1,0:T(8,128)(2,1)} %wo_ref.1, s32[1]{0:T(128)S(6)} %copy.15.step_ref, ...), custom_call_target="tpu_custom_call" | custom-call | tf_op jit(solution)/shard_map/step/pallas_call | solution.py:917
  118.2 1.3 %slice_reduce_fusion = f32[4]{0:T(128)} fusion(f32[8,128]{1,0:T(8,128)} %get-tuple-element.5), kind=kLoop, calls=%fused_computation | loop fusion | bytes 32 | tf_op jit(solution)/shard_map/slice | solution.py:972
  119.5 2.1 %copy.16 = bf16[4,64,1536]{2,1,0:T(8,128)(2,1)} copy(bf16[4,64,1536]{2,1,0:T(8,128)(2,1)} %get-tuple-element.8) | data formatting | bytes 1572864

commit v2 on v1

--- a/solution.py
+++ b/solution.py
@@ -247,15 +247,12 @@
         else:
             each_arrival(step, action)
 
-    def weight_step(step):
+    def move_step(step):
         if 1 <= step < length:
             line_step(step)
         if 0 <= step - 1 < length:
             fan_step(step - 1)
-        if 0 <= step - 2 < length:
-            group_step(step - 2)
-
-    weight_steps = length + 2
+
 
     def finish_weights(parts=(0, 1)):
         for which in parts:
@@ -282,7 +279,217 @@
                         dom_copy(which, owner, shift, group_shift, True).wait_recv()
                         dom_copy(which, owner, shift, group_shift, False).wait_send()
 
-    return line_start, weight_step, finish_weights, weight_steps
+    return line_start, move_step, group_step, finish_weights, length
+
+
+def take(semaphore, region):
+    pltpu.make_async_copy(region, region, semaphore).wait()
+
+
+def shared_weight_exchange(
+    n, fan, group_count, dom_count, embed_ref, up_ref, embed_full, up_full,
+    shard_own, line_send, line_recv, fan_send, fan_recv, group_send, group_recv, dom_send, dom_recv,
+):
+    me = lax.axis_index("seq")
+    my_group = lax.axis_index("groups")
+    my_dom = lax.axis_index("dom")
+    share_count = group_count * dom_count
+    embed_rows, embed_cols = embed_ref.shape
+    up_rows, up_cols = up_ref.shape
+    embed_part = embed_cols // share_count
+    up_part = up_rows // share_count
+
+    def share(which, owner, group, dom, own=False):
+        part = group * dom_count + dom
+        if which == 0:
+            columns = pl.ds(pl.multiple_of(part * embed_part, LANES), embed_part)
+            if own:
+                return embed_ref.at[:, columns]
+            return embed_full.at[
+                pl.ds(pl.multiple_of(owner * embed_rows, 16), embed_rows), columns
+            ]
+        rows = pl.ds(pl.multiple_of(part * up_part, 16), up_part)
+        if own:
+            return up_ref.at[rows, :]
+        return up_full.at[rows, pl.ds(pl.multiple_of(owner * up_cols, LANES), up_cols)]
+
+    def shard_copy(which):
+        if which == 0:
+            target = embed_full.at[pl.ds(pl.multiple_of(me * embed_rows, 16), embed_rows), :]
+            return pltpu.make_async_copy(embed_ref, target, shard_own.at[0])
+        target = up_full.at[:, pl.ds(pl.multiple_of(me * up_cols, LANES), up_cols)]
+        return pltpu.make_async_copy(up_ref, target, shard_own.at[1])
+
+    place = lax.div(me, fan)
+    lane = lax.rem(me, fan)
+    length = n // fan
+    signs = (1, -1)
+
+    def line_copy(which, direction, step, incoming):
+        sign = signs[direction]
+        origin = place - sign * (step if incoming else step - 1)
+        owner = lax.rem(origin + n, length) * fan + lane
+        to = lax.rem(place + sign + n, length) * fan + lane
+        return pltpu.make_async_remote_copy(
+            src_ref=share(which, owner, my_group, my_dom, own=step == 1 and not incoming),
+            dst_ref=share(which, owner, my_group, my_dom),
+            send_sem=line_send.at[which, direction, step - 1],
+            recv_sem=line_recv.at[which, direction, step - 1],
+            device_id={"seq": to},
+            device_id_type=MESH,
+        )
+
+    def receives(direction, step):
+        return place >= step if direction == 0 else place + step < length
+
+    def sends(direction, step):
+        if direction == 0:
+            return jnp.logical_and(place >= step - 1, place + 1 < length)
+        return jnp.logical_and(place + step - 1 < length, place >= 1)
+
+    def fan_copy(which, spot, shift, incoming, own=False):
+        to = lax.rem(lane + shift, fan)
+        source = lax.rem(lane - shift + fan, fan) if incoming else lane
+        owner = spot * fan + source
+        return pltpu.make_async_remote_copy(
+            src_ref=share(which, owner, my_group, my_dom, own=own),
+            dst_ref=share(which, owner, my_group, my_dom),
+            send_sem=fan_send.at[which, shift - 1],
+            recv_sem=fan_recv.at[which, shift - 1, spot],
+            device_id={"seq": place * fan + to},
+            device_id_type=MESH,
+        )
+
+    def group_copy(which, owner, shift, incoming):
+        other = lax.rem(my_group + shift, group_count)
+        source = lax.rem(my_group - shift + group_count, group_count) if incoming else my_group
+        return pltpu.make_async_remote_copy(
+            src_ref=share(which, owner, source, my_dom),
+            dst_ref=share(which, owner, source, my_dom),
+            send_sem=group_send.at[which, shift - 1],
+            recv_sem=group_recv.at[which, shift - 1, owner],
+            device_id={"groups": other},
+            device_id_type=MESH,
+        )
+
+    def dom_copy(which, owner, shift, group_shift, incoming):
+        other = lax.rem(my_dom + shift, dom_count)
+        source = lax.rem(my_dom - shift + dom_count, dom_count) if incoming else my_dom
+        group = lax.rem(my_group - group_shift + group_count, group_count)
+        return pltpu.make_async_remote_copy(
+            src_ref=share(which, owner, group, source),
+            dst_ref=share(which, owner, group, source),
+            send_sem=dom_send.at[which, shift - 1],
+            recv_sem=dom_recv.at[which, shift - 1],
+            device_id={"dom": other},
+            device_id_type=MESH,
+        )
+
+    def spread(which, owner):
+        for shift in range(1, group_count):
+            group_copy(which, owner, shift, False).start()
+        for shift in range(1, dom_count):
+            dom_copy(which, owner, shift, 0, False).start()
+
+    def each_arrival(step, action):
+        for direction in range(2):
+
+            @pl.when(receives(direction, step))
+            def _(direction=direction):
+                for which in range(2):
+                    action(which, direction, place - signs[direction] * step)
+
+    def line_start():
+        for which in range(2):
+            for direction in range(2):
+
+                @pl.when(sends(direction, 1))
+                def _(which=which, direction=direction):
+                    line_copy(which, direction, 1, False).start()
+
+            for shift in range(1, fan):
+                fan_copy(which, place, shift, False, own=True).start()
+            shard_copy(which).start()
+
+    def line_step(step):
+        def action(which, direction, spot):
+            line_copy(which, direction, step, True).wait_recv()
+            if step + 1 < length:
+
+                @pl.when(sends(direction, step + 1))
+                def _():
+                    line_copy(which, direction, step + 1, False).start()
+
+            for shift in range(1, fan):
+                fan_copy(which, spot, shift, False).start()
+            spread(which, spot * fan + lane)
+
+        each_arrival(step, action)
+
+    def fan_step(step):
+        def action(which, direction, spot):
+            for shift in range(1, fan):
+                fan_copy(which, spot, shift, True).wait_recv()
+                spread(which, spot * fan + lax.rem(lane - shift + fan, fan))
+
+        if step == 0:
+            for which in range(2):
+                action(which, 0, place)
+        else:
+            each_arrival(step, action)
+
+    def group_block(which, owner):
+        for group_shift in range(1, group_count):
+            group_copy(which, owner, group_shift, True).wait_recv()
+            for shift in range(1, dom_count):
+                dom_copy(which, owner, shift, group_shift, False).start()
+
+    def group_step(step):
+        def action(which, direction, spot):
+            if step > 0:
+                group_block(which, spot * fan + lane)
+            for shift in range(1, fan):
+                group_block(which, spot * fan + lax.rem(lane - shift + fan, fan))
+
+        if step == 0:
+            for which in range(2):
+                action(which, 0, place)
+        else:
+            each_arrival(step, action)
+
+    def move_step(step):
+        if 1 <= step < length:
+            line_step(step)
+        if 0 <= step - 1 < length:
+            fan_step(step - 1)
+
+
+    def parts_of(which, amount):
+        if which == 0:
+            wide = math.gcd(amount, share_count)
+            return embed_full.at[0 : amount // wide * embed_rows, 0 : wide * embed_part]
+        wide = math.gcd(amount, share_count)
+        return up_full.at[0 : wide * up_part, 0 : amount // wide * up_cols]
+
+    def finish_weights(parts=(0, 1)):
+        for which in parts:
+            shard_copy(which).wait()
+            for direction in range(2):
+                for step in range(1, length):
+
+                    @pl.when(sends(direction, step))
+                    def _(which=which, direction=direction, step=step):
+                        line_copy(which, direction, step, False).wait_send()
+
+            for shift in range(1, fan):
+                take(fan_send.at[which, shift - 1], parts_of(which, length))
+            for shift in range(1, group_count):
+                take(group_send.at[which, shift - 1], parts_of(which, n - 1))
+            for shift in range(1, dom_count):
+                take(dom_recv.at[which, shift - 1], parts_of(which, (n - 1) * group_count))
+                take(dom_send.at[which, shift - 1], parts_of(which, (n - 1) * group_count))
+
+    return line_start, move_step, group_step, finish_weights, length
 
 
 def attention_kernel(
@@ -315,7 +522,7 @@
         pl.semaphore_signal(barrier, inc=1, device_id=peer, device_id_type=MESH)
     pl.semaphore_wait(barrier, n - 1 + group_count - 1 + dom_count - 1)
 
-    line_start, weight_step, finish_weights, weight_steps = weight_exchange(
+    line_start, move_step, group_step, finish_weights, length = weight_exchange(
         n, fan, group_count, dom_count, embed_ref, up_ref, embed_full, up_full,
         shard_own, line_send, line_recv, fan_send, fan_recv, group_send, group_recv,
         dom_send, dom_recv,
@@ -360,6 +567,13 @@
             piece(o_ref, me, groups, cols, chunk * width, width),
             back_own.at[chunk],
         )
+
+    weight_steps = length + 2
+
+    def weight_step(step):
+        move_step(step)
+        if 0 <= step - 2 < length:
+            group_step(step - 2)
 
     ready = 1
     for chunk in range(chunks):
@@ -590,12 +804,13 @@
 
 
 def fused_kernel(
-    n, fan, group_count, dom_count, groups, chunks, head_width, row_block, tile,
-    q_ref, k_ref, v_ref, lat_ref, wo_ref, step_ref, embed_ref, gain_ref, up_ref, head_ref,
-    prev_ref, anc_ref, out_ref, logw_ref,
+    n, fan, group_count, dom_count, rounds, groups, chunks, head_width, row_block, tile,
+    q_ref, k_ref, v_ref, lat_ref, wo_ref, step_in, embed_ref, gain_in, up_ref, head_in,
+    prev_in, anc_in, out_ref, logw_ref,
+    step_ref, gain_ref, head_ref, prev_ref, anc_ref, picked,
     qb, kb, vb, ob, mixed, embed_full, up_full, wo, lat, velocity, clean, embedded, features,
     cand, score, mine, held,
-    send_sem, recv_sem, own_sem, back_send, back_recv, back_own,
+    send_sem, recv_sem, back_send, back_recv,
     shard_own, line_send, line_recv, fan_send, fan_recv, group_send, group_recv, dom_send, dom_recv,
     load_sem, step_send, step_recv, score_send, score_recv,
 ):
@@ -604,7 +819,8 @@
     my_dom = lax.axis_index("dom")
     particles, tokens, model_width = q_ref.shape
     rows = particles * tokens
-    cols = model_width // groups
+    share = particles // rounds
+    share_rows = share * tokens
     total_tokens = n * tokens
     inputs = ((q_ref, qb), (k_ref, kb), (v_ref, vb))
     members = n * dom_count
@@ -614,10 +830,14 @@
         other = lax.rem(member + step, members)
         return other, {"dom": other // n, "seq": other % n}
 
-    loads = (
-        pltpu.make_async_copy(wo_ref, wo, load_sem.at[0]),
-        pltpu.make_async_copy(lat_ref, lat, load_sem.at[1]),
+    small = (
+        (wo_ref, wo), (lat_ref, lat), (step_in, step_ref), (gain_in, gain_ref),
+        (head_in, head_ref), (prev_in, prev_ref), (anc_in, anc_ref),
     )
+    loads = [
+        pltpu.make_async_copy(source, target, load_sem.at[at])
+        for at, (source, target) in enumerate(small)
+    ]
 
     barrier = pltpu.get_barrier_semaphore()
 
@@ -633,35 +853,37 @@
         load.start()
     pl.semaphore_wait(barrier, members - 1 + group_count - 1)
 
-    line_start, weight_step, finish_weights, weight_steps = weight_exchange(
+    line_start, move_step, group_step, finish_weights, length = shared_weight_exchange(
         n, fan, group_count, dom_count, embed_ref, up_ref, embed_full, up_full,
         shard_own, line_send, line_recv, fan_send, fan_recv, group_send, group_recv,
         dom_send, dom_recv,
     )
 
+    cols = model_width // groups
+
     def source_of(ref, item, chunk):
-        start, width = chunks[chunk]
+        turn, start, width = chunks[chunk]
         offset = pl.multiple_of(groups * start + (item % groups) * width, LANES)
-        return ref.at[item // groups, :, pl.ds(offset, width)]
+        return ref.at[turn * share + item // groups, :, pl.ds(offset, width)]
 
     def mixed_of(item, chunk):
-        start, width = chunks[chunk]
+        turn, start, width = chunks[chunk]
         offset = pl.multiple_of(groups * start + (item % groups) * width, LANES)
-        row = pl.multiple_of((item // groups) * tokens, 16)
+        row = pl.multiple_of((turn * share + item // groups) * tokens, 16)
         return mixed.at[pl.ds(row, tokens), pl.ds(offset, width)]
 
     def rows_of(ref, owner, chunk):
-        start, width = chunks[chunk]
+        turn, start, width = chunks[chunk]
         row = pl.ds(pl.multiple_of(owner * tokens, 16), tokens)
-        return ref.at[row, pl.ds(start, width)]
-
-    def outgoing(index, chunk, target, slot):
+        return ref.at[row, pl.ds(turn * cols + start, width)]
+
+    def outgoing(index, chunk, target):
         source, buffer = inputs[index]
         return pltpu.make_async_remote_copy(
             src_ref=source_of(source, target, chunk),
             dst_ref=rows_of(buffer, me, chunk),
-            send_sem=send_sem.at[index, chunk, target],
-            recv_sem=recv_sem.at[index, chunk, slot],
+            send_sem=send_sem.at[index, chunk],
+            recv_sem=recv_sem.at[index, chunk],
             device_id={"seq": target},
             device_id_type=MESH,
         )
@@ -669,145 +891,154 @@
     def own_copy(index, chunk):
         source, buffer = inputs[index]
         return pltpu.make_async_copy(
-            source_of(source, me, chunk), rows_of(buffer, me, chunk), own_sem.at[index, chunk]
-        )
-
-    def returned(chunk, target, slot):
+            source_of(source, me, chunk), rows_of(buffer, me, chunk), recv_sem.at[index, chunk]
+        )
+
+    def returned(chunk, target):
         return pltpu.make_async_remote_copy(
             src_ref=rows_of(ob, target, chunk),
             dst_ref=mixed_of(me, chunk),
-            send_sem=back_send.at[chunk, target],
-            recv_sem=back_recv.at[chunk, slot],
+            send_sem=back_send.at[chunk],
+            recv_sem=back_recv.at[chunk],
             device_id={"seq": target},
             device_id_type=MESH,
         )
 
     def own_return(chunk):
         return pltpu.make_async_copy(
-            rows_of(ob, me, chunk), mixed_of(me, chunk), back_own.at[chunk]
+            rows_of(ob, me, chunk), mixed_of(me, chunk), back_recv.at[chunk]
         )
 
     count = len(chunks)
-    ready = 1
-    for chunk in range(count):
-        if chunk == 0:
-            line_start()
-        elif ready < weight_steps:
-            weight_step(ready)
-            ready += 1
+    blocks = total_tokens // row_block
+
+    def issue(chunk):
         for index in range(3):
             own_copy(index, chunk).start()
 
             @pl.loop(1, n)
-            def _(step, index=index, chunk=chunk):
-                outgoing(index, chunk, lax.rem(me + step, n), me).start()
-
-    blocks = total_tokens // row_block
-
-    for chunk in range(count):
-        start, width = chunks[chunk]
-        for index in range(3):
-            own_copy(index, chunk).wait()
-
-            @pl.loop(1, n)
-            def _(step, index=index, chunk=chunk):
-                other = lax.rem(me + step, n)
-                outgoing(index, chunk, other, other).wait_recv()
+            def _(step, index=index):
+                outgoing(index, chunk, lax.rem(me + step, n)).start()
+
+    def attend(chunk):
+        turn, start, width = chunks[chunk]
+        first = turn * cols + start
 
         @pl.loop(0, (width // LANES) * blocks)
-        def _(step, start=start):
+        def _(step):
             attend_pair(
                 qb, kb, vb, ob,
                 pl.multiple_of((step % blocks) * row_block, row_block), row_block,
-                start + (step // blocks) * LANES, head_width,
+                first + (step // blocks) * LANES, head_width,
             )
 
+    def arrive(chunk):
+        turn, start, width = chunks[chunk]
+        for index in range(3):
+            buffer = inputs[index][1]
+            first = turn * cols + start
+            take(recv_sem.at[index, chunk], buffer.at[:, first : first + width])
+
+    def give_back(chunk):
         own_return(chunk).start()
 
         @pl.loop(1, n)
-        def _(step, chunk=chunk):
-            returned(chunk, lax.rem(me + step, n), me).start()
-
-        if ready < weight_steps and chunk < count - 1:
-            weight_step(ready)
-            ready += 1
-
-    for step in range(ready, weight_steps):
-        weight_step(step)
-    for load in loads:
-        load.wait()
-
-    sigma = step_ref[0].astype(jnp.float32) / STEPS
-
-    for chunk in range(count):
-        start, width = chunks[chunk]
+        def _(step):
+            returned(chunk, lax.rem(me + step, n)).start()
+
+    def project(chunk):
+        if chunk == 0:
+            for load in loads:
+                load.wait()
+        sigma = step_ref[0].astype(jnp.float32) / STEPS
+        turn, start, width = chunks[chunk]
         inner = pl.ds(groups * start, groups * width)
-        own_return(chunk).wait()
-
-        @pl.loop(1, n)
-        def _(step, chunk=chunk):
-            other = lax.rem(me + step, n)
-            returned(chunk, other, other).wait_recv()
+        own_rows = pl.ds(turn * share_rows, share_rows)
+        final = chunk + 1 == count or chunks[chunk + 1][0] != turn
+        take(back_recv.at[chunk], mixed.at[own_rows, inner])
 
         @pl.loop(0, model_width // tile)
-        def _(step, chunk=chunk, inner=inner):
+        def _(step):
             columns = pl.ds(pl.multiple_of(step * tile, tile), tile)
-            part = jnp.dot(mixed[:, inner], wo[inner, columns], preferred_element_type=jnp.float32)
-            if chunk > 0:
-                part = velocity[:, columns] + part
-            if chunk < count - 1:
-                velocity[:, columns] = part
+            part = jnp.dot(
+                mixed[own_rows, inner], wo[inner, columns], preferred_element_type=jnp.float32
+            )
+            if start > 0:
+                part = velocity[own_rows, columns] + part
+            if not final:
+                velocity[own_rows, columns] = part
                 return
-            flat = lat[:, :, columns].reshape(rows, tile).astype(jnp.float32)
-            moved = flat + part
-            clean[:, columns] = (flat - sigma * moved).astype(jnp.bfloat16)
-            stepped = (flat - moved / STEPS).astype(jnp.bfloat16)
-            for item in range(particles):
-                cand[my_dom * particles + item, :, columns] = stepped[
-                    item * tokens : (item + 1) * tokens
-                ]
-
-    finish_weights((0,))
-
-    @pl.loop(0, embedded.shape[1] // tile)
-    def _(step):
-        columns = pl.ds(pl.multiple_of(step * tile, tile), tile)
-        embedded[:, columns] = jnp.dot(
-            clean[...], embed_full[:, columns], preferred_element_type=jnp.float32
-        )
-
-    def step_copy(shift, incoming):
+            for item in range(share):
+                at = slice(item * tokens, (item + 1) * tokens)
+                spot = turn * share + item
+                flat = lat[spot, :, columns].astype(jnp.float32)
+                moved = flat + part[at]
+                clean[spot * tokens : (spot + 1) * tokens, columns] = (
+                    flat - sigma * moved
+                ).astype(jnp.bfloat16)
+                cand[my_dom * particles + spot, :, columns] = (flat - moved / STEPS).astype(
+                    jnp.bfloat16
+                )
+
+    def step_copy(turn, shift, incoming):
         source = lax.rem(my_dom - shift + dom_count, dom_count) if incoming else my_dom
-        block = cand.at[pl.ds(source * particles, particles)]
+        block = cand.at[pl.ds(source * particles + turn * share, share)]
         return pltpu.make_async_remote_copy(
             src_ref=block,
             dst_ref=block,
-            send_sem=step_send.at[shift],
-            recv_sem=step_recv.at[shift],
+            send_sem=step_send.at[turn, shift - 1],
+            recv_sem=step_recv.at[turn, shift - 1],
             device_id={"dom": lax.rem(my_dom + shift, dom_count)},
             device_id_type=MESH,
         )
 
-    for shift in range(1, dom_count):
-        step_copy(shift, False).start()
-
-    @pl.loop(0, particles)
-    def _(item):
-        own_rows = pl.ds(pl.multiple_of(item * tokens, tokens), tokens)
-        block = embedded[own_rows, :]
-        centered = block - jnp.mean(block, axis=1, keepdims=True)
-        variance = jnp.mean(centered * centered, axis=1, keepdims=True)
-        normed = centered * lax.rsqrt(variance + norm_eps) * gain_ref[...]
-        features[own_rows, :] = jax.nn.gelu(normed).astype(jnp.bfloat16)
-
-    finish_weights((1,))
+    def embed(turn):
+        if turn == 0:
+            finish_weights((0,))
+        own_rows = pl.ds(turn * share_rows, share_rows)
+
+        @pl.loop(0, embedded.shape[1] // tile)
+        def _(step):
+            columns = pl.ds(pl.multiple_of(step * tile, tile), tile)
+            embedded[own_rows, columns] = jnp.dot(
+                clean[own_rows, :], embed_full[:, columns], preferred_element_type=jnp.float32
+            )
+
+        for shift in range(1, dom_count):
+            step_copy(turn, shift, False).start()
+
+        @pl.loop(turn * share, (turn + 1) * share)
+        def _(item):
+            item_rows = pl.ds(pl.multiple_of(item * tokens, tokens), tokens)
+            block = embedded[item_rows, :]
+            centered = block - jnp.mean(block, axis=1, keepdims=True)
+            variance = jnp.mean(centered * centered, axis=1, keepdims=True)
+            normed = centered * lax.rsqrt(variance + norm_eps) * gain_ref[...]
+            features[item_rows, :] = jax.nn.gelu(normed).astype(jnp.bfloat16)
+
+    def judge(turn):
+        if turn == 0:
+            finish_weights((1,))
+        own_rows = pl.ds(turn * share_rows, share_rows)
+
+        @pl.loop(0, up_full.shape[1] // tile)
+        def _(step):
+            columns = pl.ds(pl.multiple_of(step * tile, tile), tile)
+            hidden = jnp.dot(
+                features[own_rows, :], up_full[:, columns], preferred_element_type=jnp.float32
+            )
+            score[turn * share : (turn + 1) * share, :] += (
+                part_sum(jax.nn.gelu(hidden), tokens) * head_ref[:, columns]
+            )
+
+    actions = {
+        "issue": issue, "arrive": arrive, "attend": attend, "return": give_back,
+        "move": move_step, "group": group_step, "line": lambda _: line_start(),
+        "project": project, "embed": embed, "judge": judge,
+    }
     score[...] = jnp.zeros_like(score)
-
-    @pl.loop(0, up_full.shape[1] // tile)
-    def _(step):
-        columns = pl.ds(pl.multiple_of(step * tile, tile), tile)
-        hidden = jnp.dot(features[...], up_full[:, columns], preferred_element_type=jnp.float32)
-        score[...] += part_sum(jax.nn.gelu(hidden), tokens) * head_ref[:, columns]
+    for name, at in plan(chunks, length):
+        actions[name](at)
 
     partial_value = jnp.sum(score[...], axis=1, keepdims=True) / math.sqrt(total_tokens)
     lane = lax.broadcasted_iota(jnp.int32, (particles, LANES), 1)
@@ -820,43 +1051,40 @@
     mine[0:particles, :] = own_block
     held[member, 0:particles, :] = own_block
 
-    def score_copy(step, slot):
-        other, device = other_member(step)
+    def score_copy(step):
+        _, device = other_member(step)
         return pltpu.make_async_remote_copy(
             src_ref=mine,
             dst_ref=held.at[member],
-            send_sem=score_send.at[other],
-            recv_sem=score_recv.at[slot],
+            send_sem=score_send.at[0],
+            recv_sem=score_recv.at[0],
             device_id=device,
             device_id_type=MESH,
         )
 
     @pl.loop(1, members)
     def _(step):
-        score_copy(step, member).start()
-
-    for shift in range(1, dom_count):
-        step_copy(shift, True).wait_recv()
+        score_copy(step).start()
+
+    for turn in range(rounds):
+        for shift in range(1, dom_count):
+            step_copy(turn, shift, True).wait_recv()
     for item in range(particles):
-        out_ref[item] = cand[anc_ref[item]]
+        picked[item] = cand[anc_ref[item]]
+    write = pltpu.make_async_copy(picked, out_ref, load_sem.at[0])
+    write.start()
 
     for chunk in range(count):
+        sent = qb.at[0 : (n - 1) * tokens, 0 : chunks[chunk][2]]
         for index in range(3):
-
-            @pl.loop(1, n)
-            def _(step, index=index, chunk=chunk):
-                outgoing(index, chunk, lax.rem(me + step, n), me).wait_send()
-
-        @pl.loop(1, n)
-        def _(step, chunk=chunk):
-            returned(chunk, lax.rem(me + step, n), me).wait_send()
-
-    for shift in range(1, dom_count):
-        step_copy(shift, False).wait_send()
-
-    @pl.loop(1, members)
-    def _(step):
-        score_copy(step, lax.rem(member + step, members)).wait_recv()
+            take(send_sem.at[index, chunk], sent)
+        take(back_send.at[chunk], sent)
+
+    for turn in range(rounds):
+        for shift in range(1, dom_count):
+            step_copy(turn, shift, False).wait_send()
+
+    take(score_recv.at[0], held.at[0 : members - 1])
 
     logits = []
     for dom in range(dom_count):
@@ -873,20 +1101,50 @@
         own - (highest + jnp.log(total)), (particles, LANES)
     )
 
-    @pl.loop(1, members)
-    def _(step):
-        score_copy(step, member).wait_send()
-
-
-def chunk_widths(cols):
-    widths = []
-    left = cols
-    while left > 2 * LANES + LANES:
-        widths.append(2 * LANES)
-        left -= 2 * LANES
-    widths += [LANES] * (left // LANES)
-    starts = [sum(widths[:i]) for i in range(len(widths))]
-    return tuple(zip(starts, widths))
+    take(score_send.at[0], held.at[0 : members - 1])
+    write.wait()
+
+
+def plan(chunks, length):
+    count = len(chunks)
+    steps = [("line", 0), ("issue", 0), ("move", 1)] + [("issue", at) for at in range(1, count)][:1]
+    moved, grouped, projected = 1, 0, 0
+    for chunk in range(count):
+        steps += [("arrive", chunk), ("attend", chunk), ("return", chunk)]
+        if moved < length:
+            moved += 1
+            steps.append(("move", moved))
+        if chunk + 2 < count:
+            steps.append(("issue", chunk + 2))
+        if chunk + 2 == count:
+            steps += [("move", step) for step in range(moved + 1, length + 1)]
+            moved = length
+            steps += [("group", step) for step in range(length)]
+            grouped = length
+            while chunks[projected][0] < chunks[-1][0]:
+                steps.append(("project", projected))
+                projected += 1
+    steps += [("move", step) for step in range(moved + 1, length + 1)]
+    steps += [("group", step) for step in range(grouped, length)]
+    for chunk in range(projected):
+        turn = chunks[chunk][0]
+        if chunks[chunk + 1][0] > turn:
+            steps += [("embed", turn), ("judge", turn)]
+    steps += [("project", chunk) for chunk in range(projected, count)]
+    return steps + [("embed", chunks[-1][0]), ("judge", chunks[-1][0])]
+
+
+def chunk_list(rounds, cols):
+    chunks = []
+    for turn in range(rounds):
+        widths = [2 * LANES] * (cols // (2 * LANES)) + [LANES] * (cols % (2 * LANES) // LANES)
+        if turn == 0:
+            widths.reverse()
+        start = 0
+        for width in widths:
+            chunks.append((turn, start, width))
+            start += width
+    return tuple(chunks)
 
 
 def fused(
@@ -899,33 +1157,42 @@
     fan = 2 if n % 2 == 0 else 1
     particles, tokens, model_width = queries.shape
     head_width = model_width // HEADS
-    cols = particles * model_width // n
+    rounds = round_count(n, particles, model_width)
+    cols = particles * model_width // (n * rounds)
     groups = model_width // cols
-    chunks = chunk_widths(cols)
+    chunks = chunk_list(rounds, cols)
     count = len(chunks)
     rows = particles * tokens
     total_tokens = n * tokens
     members = n * dom_count
+    fan_steps, group_steps, dom_steps = (max(x - 1, 1) for x in (fan, group_count, dom_count))
     tile = 512
     embed_shape = (n * embed_weight.shape[0], embed_weight.shape[1])
     up_shape = (up_weight.shape[0], n * up_weight.shape[1])
     hbm = pl.BlockSpec(memory_space=pl.ANY)
     vmem = pl.BlockSpec(memory_space=pltpu.VMEM)
-    smem = pl.BlockSpec(memory_space=pltpu.SMEM)
     bf16 = jnp.bfloat16
     dma = pltpu.SemaphoreType.DMA
     resampled, logw = pl.pallas_call(
         functools.partial(
-            fused_kernel, n, fan, group_count, dom_count, groups, chunks, head_width,
+            fused_kernel, n, fan, group_count, dom_count, rounds, groups, chunks, head_width,
             min(256, total_tokens), tile,
         ),
         out_shape=(
             jax.ShapeDtypeStruct(latents.shape, bf16),
             jax.ShapeDtypeStruct((8, LANES), jnp.float32),
         ),
-        in_specs=[hbm] * 5 + [smem, hbm, vmem, hbm, vmem, smem, smem],
-        out_specs=(vmem, vmem),
-        scratch_shapes=[pltpu.VMEM((total_tokens, cols), bf16)] * 4
+        in_specs=[hbm] * 12,
+        out_specs=(hbm, vmem),
+        scratch_shapes=[
+            pltpu.SMEM(step_index.shape, jnp.int32),
+            pltpu.VMEM((1, norm_gain.shape[0]), jnp.float32),
+            pltpu.VMEM((1, head_weight.shape[0]), jnp.float32),
+            pltpu.SMEM(prev_logw.shape, jnp.float32),
+            pltpu.SMEM(ancestors.shape, jnp.int32),
+            pltpu.VMEM(latents.shape, bf16),
+        ]
+        + [pltpu.VMEM((total_tokens, rounds * cols), bf16)] * 4
         + [
             pltpu.VMEM((rows, model_width), bf16),
             pltpu.VMEM(embed_shape, bf16),
@@ -940,26 +1207,24 @@
             pltpu.VMEM((particles, tile), jnp.float32),
             pltpu.VMEM((8, LANES), jnp.float32),
             pltpu.VMEM((members, 8, LANES), jnp.float32),
-            dma((3, count, n)),
-            dma((3, count, n)),
             dma((3, count)),
-            dma((count, n)),
-            dma((count, n)),
+            dma((3, count)),
+            dma((count,)),
             dma((count,)),
             dma((2,)),
-            dma((2, 2, n // fan)),
-            dma((2, 2, n // fan)),
-            dma((2, fan, n // fan)),
-            dma((2, fan, n // fan)),
-            dma((2, group_count, n)),
-            dma((2, group_count, n)),
-            dma((2, dom_count, group_count, n)),
-            dma((2, dom_count, group_count, n)),
-            dma((2,)),
-            dma((dom_count,)),
-            dma((dom_count,)),
-            dma((members,)),
-            dma((members,)),
+            dma((2, 2, max(n // fan - 1, 1))),
+            dma((2, 2, max(n // fan - 1, 1))),
+            dma((2, fan_steps)),
+            dma((2, fan_steps, n // fan)),
+            dma((2, group_steps)),
+            dma((2, group_steps, n)),
+            dma((2, dom_steps)),
+            dma((2, dom_steps)),
+            dma((7,)),
+            dma((rounds, dom_steps)),
+            dma((rounds, dom_steps)),
+            dma((1,)),
+            dma((1,)),
         ],
         compiler_params=pltpu.CompilerParams(
             collective_id=0, has_side_effects=True, vmem_limit_bytes=60 * 1024 * 1024
@@ -972,13 +1237,20 @@
     return resampled, logw[:particles, 0]
 
 
+def round_count(n, particles, model_width):
+    for rounds in (2, 1):
+        if particles % rounds or (particles * HEADS) % (n * rounds):
+            continue
+        cols = particles * model_width // (n * rounds)
+        if cols % LANES == 0 and model_width % cols == 0:
+            return rounds
+    return 0
+
+
 def tiles_evenly(queries, embed_weight, up_weight):
     n = lax.axis_size("seq")
     particles, tokens, model_width = queries.shape
-    if particles * HEADS % n:
-        return False
-    cols = particles * model_width // n
-    if 2 * (model_width // HEADS) != LANES or cols % LANES or model_width % cols:
+    if 2 * (model_width // HEADS) != LANES or not round_count(n, particles, model_width):
         return False
     return model_width % 512 == 0 and embed_weight.shape[1] % 512 == 0
 

time: 122 us -> 114 us (0.934)
  Pallas kernels: 117 us -> 109 us
    pallas_call x1, Pallas kernels: 117 us -> 109 us  [fused(): pl.pallas_call(functools.partial(fused_kernel, n, fan, group_count, dom_c...]
where the time goes in v2:
time: 114 us
  Pallas kernels  109 us (96%)
  local copies, waits for them, and re-layouts  3.36 us (3%)
  between operations  1.29 us (1%)
    pallas_call x1, Pallas kernels, fused(): pl.pallas_call(functools.partial(fused_kernel, n, fan, group_count, dom_c...  109 us

profile of v2, /device:TPU:0, one launch (start us, length us, event | category | flops | bytes accessed | tf_op | source)
XLA Modules:
  0.0 113.8 jit_solution(10286972541743387533)
XLA Ops:
  1.3 109.2 %step.1 = (bf16[4,64,1536]{2,1,0:T(8,128)(2,1)}, f32[8,128]{1,0:T(8,128)}) custom-call(bf16[4,64,1536]{2,1,0:T(8,128)(2,1)} %q_ref.1, bf16[4,64,1536]{2,1,0:T(8,128)(2,1)} %k_ref.1, bf16[4,64,1536]{2,1,0:T(8,128)(2,1)} %v_ref.1, bf16[4,64,1536]{2,1,0:T(8,128)(2,1)} %lat_ref.1, bf16[1536,1536]{1,0:T(8,128)(2,1)} %wo_ref.1, s32[1]{0:T(128)S(6)} %copy.15.step_in, ...), custom_call_target="tpu_custom_call" | custom-call | tf_op jit(solution)/shard_map/step/pallas_call | solution.py:1176
  110.5 1.3 %slice_reduce_fusion = f32[4]{0:T(128)} fusion(f32[8,128]{1,0:T(8,128)} %get-tuple-element.5), kind=kLoop, calls=%fused_computation | loop fusion | bytes 32 | tf_op jit(solution)/shard_map/slice | solution.py:1237
  111.8 2.1 %copy.16 = bf16[4,64,1536]{2,1,0:T(8,128)(2,1)} copy(bf16[4,64,1536]{2,1,0:T(8,128)(2,1)} %get-tuple-element.8) | data formatting | bytes 1572864

commit v3 on v2

--- a/solution.py
+++ b/solution.py
@@ -457,13 +457,6 @@
         else:
             each_arrival(step, action)
 
-    def move_step(step):
-        if 1 <= step < length:
-            line_step(step)
-        if 0 <= step - 1 < length:
-            fan_step(step - 1)
-
-
     def parts_of(which, amount):
         if which == 0:
             wide = math.gcd(amount, share_count)
@@ -489,7 +482,7 @@
                 take(dom_recv.at[which, shift - 1], parts_of(which, (n - 1) * group_count))
                 take(dom_send.at[which, shift - 1], parts_of(which, (n - 1) * group_count))
 
-    return line_start, move_step, group_step, finish_weights, length
+    return line_start, line_step, fan_step, group_step, finish_weights, length
 
 
 def attention_kernel(
@@ -853,7 +846,7 @@
         load.start()
     pl.semaphore_wait(barrier, members - 1 + group_count - 1)
 
-    line_start, move_step, group_step, finish_weights, length = shared_weight_exchange(
+    line_start, line_step, fan_step, group_step, finish_weights, length = shared_weight_exchange(
         n, fan, group_count, dom_count, embed_ref, up_ref, embed_full, up_full,
         shard_own, line_send, line_recv, fan_send, fan_recv, group_send, group_recv,
         dom_send, dom_recv,
@@ -957,7 +950,7 @@
         final = chunk + 1 == count or chunks[chunk + 1][0] != turn
         take(back_recv.at[chunk], mixed.at[own_rows, inner])
 
-        @pl.loop(0, model_width // tile)
+        @pl.loop(0, model_width // tile, unroll=model_width // tile)
         def _(step):
             columns = pl.ds(pl.multiple_of(step * tile, tile), tile)
             part = jnp.dot(
@@ -997,7 +990,7 @@
             finish_weights((0,))
         own_rows = pl.ds(turn * share_rows, share_rows)
 
-        @pl.loop(0, embedded.shape[1] // tile)
+        @pl.loop(0, embedded.shape[1] // tile, unroll=embedded.shape[1] // tile)
         def _(step):
             columns = pl.ds(pl.multiple_of(step * tile, tile), tile)
             embedded[own_rows, columns] = jnp.dot(
@@ -1021,7 +1014,7 @@
             finish_weights((1,))
         own_rows = pl.ds(turn * share_rows, share_rows)
 
-        @pl.loop(0, up_full.shape[1] // tile)
+        @pl.loop(0, up_full.shape[1] // tile, unroll=min(8, up_full.shape[1] // tile))
         def _(step):
             columns = pl.ds(pl.multiple_of(step * tile, tile), tile)
             hidden = jnp.dot(
@@ -1033,7 +1026,7 @@
 
     actions = {
         "issue": issue, "arrive": arrive, "attend": attend, "return": give_back,
-        "move": move_step, "group": group_step, "line": lambda _: line_start(),
+        "line": line_step, "fan": fan_step, "group": group_step, "start": lambda _: line_start(),
         "project": project, "embed": embed, "judge": judge,
     }
     score[...] = jnp.zeros_like(score)
@@ -1107,31 +1100,32 @@
 
 def plan(chunks, length):
     count = len(chunks)
-    steps = [("line", 0), ("issue", 0), ("move", 1)] + [("issue", at) for at in range(1, count)][:1]
-    moved, grouped, projected = 1, 0, 0
+    last = chunks[-1][0]
+    early = [chunk for chunk in range(count) if chunks[chunk][0] < last]
+    late = [chunk for chunk in range(count) if chunks[chunk][0] == last]
+    lines = list(range(2, length))
+    fans = list(range(1, length))
+    steps = [("start", 0), ("issue", 0), ("line", 1), ("fan", 0)]
+    if length == 1:
+        steps = [("start", 0), ("issue", 0), ("fan", 0)]
+    steps += [("issue", chunk) for chunk in range(1, min(2, count))]
     for chunk in range(count):
+        if chunk == count - 1:
+            steps += [("line", step) for step in lines] + [("fan", step) for step in fans]
+            steps += [("group", step) for step in range(length)]
+            steps += [("project", part) for part in early]
+        elif chunk == 0:
+            steps += [("line", step) for step in lines[:1]] + [("fan", step) for step in fans[:1]]
+            lines, fans = lines[1:], fans[1:]
         steps += [("arrive", chunk), ("attend", chunk), ("return", chunk)]
-        if moved < length:
-            moved += 1
-            steps.append(("move", moved))
         if chunk + 2 < count:
             steps.append(("issue", chunk + 2))
-        if chunk + 2 == count:
-            steps += [("move", step) for step in range(moved + 1, length + 1)]
-            moved = length
-            steps += [("group", step) for step in range(length)]
-            grouped = length
-            while chunks[projected][0] < chunks[-1][0]:
-                steps.append(("project", projected))
-                projected += 1
-    steps += [("move", step) for step in range(moved + 1, length + 1)]
-    steps += [("group", step) for step in range(grouped, length)]
-    for chunk in range(projected):
-        turn = chunks[chunk][0]
-        if chunks[chunk + 1][0] > turn:
-            steps += [("embed", turn), ("judge", turn)]
-    steps += [("project", chunk) for chunk in range(projected, count)]
-    return steps + [("embed", chunks[-1][0]), ("judge", chunks[-1][0])]
+        if chunk < count - 1:
+            steps += [("line", step) for step in lines[:1]] + [("fan", step) for step in fans[:1]]
+            lines, fans = lines[1:], fans[1:]
+    for turn in range(last):
+        steps += [("embed", turn), ("judge", turn)]
+    return steps + [("project", part) for part in late] + [("embed", last), ("judge", last)]
 
 
 def chunk_list(rounds, cols):

time: 114 us -> 106 us (0.930)
  Pallas kernels: 109 us -> 101 us
    pallas_call x1, Pallas kernels: 109 us -> 101 us  [fused(): pl.pallas_call(functools.partial(fused_kernel, n, fan, group_count, dom_c...]
where the time goes in v3:
time: 106 us
  Pallas kernels  101 us (95%)
  local copies, waits for them, and re-layouts  3.36 us (3%)
  between operations  1.29 us (1%)
    pallas_call x1, Pallas kernels, fused(): pl.pallas_call(functools.partial(fused_kernel, n, fan, group_count, dom_c...  101 us

profile of v3, /device:TPU:0, one launch (start us, length us, event | category | flops | bytes accessed | tf_op | source)
XLA Modules:
  0.0 105.9 jit_solution(5718246550018644639)
XLA Ops:
  1.3 101.2 %step.1 = (bf16[4,64,1536]{2,1,0:T(8,128)(2,1)}, f32[8,128]{1,0:T(8,128)}) custom-call(bf16[4,64,1536]{2,1,0:T(8,128)(2,1)} %q_ref.1, bf16[4,64,1536]{2,1,0:T(8,128)(2,1)} %k_ref.1, bf16[4,64,1536]{2,1,0:T(8,128)(2,1)} %v_ref.1, bf16[4,64,1536]{2,1,0:T(8,128)(2,1)} %lat_ref.1, bf16[1536,1536]{1,0:T(8,128)(2,1)} %wo_ref.1, s32[1]{0:T(128)S(6)} %copy.15.step_in, ...), custom_call_target="tpu_custom_call" | custom-call | tf_op jit(solution)/shard_map/step/pallas_call | solution.py:1170
  102.5 1.3 %slice_reduce_fusion = f32[4]{0:T(128)} fusion(f32[8,128]{1,0:T(8,128)} %get-tuple-element.5), kind=kLoop, calls=%fused_computation | loop fusion | bytes 32 | tf_op jit(solution)/shard_map/slice | solution.py:1231
  103.8 2.1 %copy.16 = bf16[4,64,1536]{2,1,0:T(8,128)(2,1)} copy(bf16[4,64,1536]{2,1,0:T(8,128)(2,1)} %get-tuple-element.8) | data formatting | bytes 1572864

commit v4 on v3

--- a/solution.py
+++ b/solution.py
@@ -1000,7 +1000,7 @@
         for shift in range(1, dom_count):
             step_copy(turn, shift, False).start()
 
-        @pl.loop(turn * share, (turn + 1) * share)
+        @pl.loop(turn * share, (turn + 1) * share, unroll=share)
         def _(item):
             item_rows = pl.ds(pl.multiple_of(item * tokens, tokens), tokens)
             block = embedded[item_rows, :]
@@ -1090,9 +1090,9 @@
     own = logits[0]
     for dom in range(1, dom_count):
         own = jnp.where(my_dom == dom, logits[dom], own)
-    logw_ref[0:particles, :] = jnp.broadcast_to(
-        own - (highest + jnp.log(total)), (particles, LANES)
-    )
+    result = jnp.broadcast_to(own - (highest + jnp.log(total)), (particles, LANES))
+    result = jnp.sum(jnp.where(row == lane, result, 0.0), axis=0, keepdims=True)
+    logw_ref[...] = result[:, 0:particles]
 
     take(score_send.at[0], held.at[0 : members - 1])
     write.wait()
@@ -1139,6 +1139,10 @@
             chunks.append((turn, start, width))
             start += width
     return tuple(chunks)
+
+
+def in_place(array):
+    return pltpu.with_memory_space_constraint(array, pltpu.HBM)
 
 
 def fused(
@@ -1174,7 +1178,7 @@
         ),
         out_shape=(
             jax.ShapeDtypeStruct(latents.shape, bf16),
-            jax.ShapeDtypeStruct((8, LANES), jnp.float32),
+            jax.ShapeDtypeStruct((1, particles), jnp.float32),
         ),
         in_specs=[hbm] * 12,
         out_specs=(hbm, vmem),
@@ -1221,14 +1225,24 @@
             dma((1,)),
         ],
         compiler_params=pltpu.CompilerParams(
-            collective_id=0, has_side_effects=True, vmem_limit_bytes=60 * 1024 * 1024
+            collective_id=0, has_side_effects=True, vmem_limit_bytes=44 * 1024 * 1024
         ),
         name="step",
     )(
-        queries, keys, values, latents, out_weight, step_index, embed_weight,
-        norm_gain.reshape(1, -1), up_weight, head_weight.reshape(1, -1), prev_logw, ancestors,
+        *map(
+            in_place,
+            (queries, keys, values, latents, out_weight),
+        ),
+        step_index,
+        *map(
+            in_place,
+            (
+                embed_weight, norm_gain.reshape(1, -1), up_weight, head_weight.reshape(1, -1),
+                prev_logw, ancestors,
+            ),
+        ),
     )
-    return resampled, logw[:particles, 0]
+    return resampled, logw[0]
 
 
 def round_count(n, particles, model_width):

time: 106 us -> 103 us (0.972)
  local copies, waits for them, and re-layouts: 3.36 us -> 1.39 us
    slice x1 -> x0, local copies, waits for them, and re-layouts: 1.3 us -> none  [fused(): return (resampled, logw[:particles, 0])]
where the time goes in v4:
time: 103 us
  Pallas kernels  100 us (97%)
  local copies, waits for them, and re-layouts  1.39 us (1%)
  between operations  1.29 us (1%)
    pallas_call x1, Pallas kernels, fused(): pl.pallas_call(functools.partial(fused_kernel, n, fan, group_count, dom_c...  100 us

profile of v4, /device:TPU:0, one launch (start us, length us, event | category | flops | bytes accessed | tf_op | source)
XLA Modules:
  0.0 103.1 jit_solution(15730550128172506399)
XLA Ops:
  1.3 100.4 %step.1 = (bf16[4,64,1536]{2,1,0:T(8,128)(2,1)S(1)}, f32[1,4]{1,0:T(1,128)S(1)}) custom-call(bf16[4,64,1536]{2,1,0:T(8,128)(2,1)} %q_ref.1, bf16[4,64,1536]{2,1,0:T(8,128)(2,1)} %k_ref.1, bf16[4,64,1536]{2,1,0:T(8,128)(2,1)} %v_ref.1, bf16[4,64,1536]{2,1,0:T(8,128)(2,1)} %lat_ref.1, bf16[1536,1536]{1,0:T(8,128)(2,1)} %wo_ref.1, s32[1]{0:T(128)S(6)} %copy.16.step_in, ...), custom_call_target="tpu_custom_call" | custom-call | tf_op jit(solution)/shard_map/step/pallas_call | solution.py:1174
  101.7 0.9 copy.17
  102.6 0.5 copy.18

commit v5 on v4

--- a/solution.py
+++ b/solution.py
@@ -904,6 +904,7 @@
 
     count = len(chunks)
     blocks = total_tokens // row_block
+    owners = row_block // tokens
 
     def issue(chunk):
         for index in range(3):
@@ -916,14 +917,22 @@
     def attend(chunk):
         turn, start, width = chunks[chunk]
         first = turn * cols + start
-
-        @pl.loop(0, (width // LANES) * blocks)
-        def _(step):
-            attend_pair(
-                qb, kb, vb, ob,
-                pl.multiple_of((step % blocks) * row_block, row_block), row_block,
-                first + (step // blocks) * LANES, head_width,
-            )
+        for at in range(1, blocks + 1):
+            block = lax.rem(lax.div(me, owners) + at, blocks)
+            row = pl.multiple_of(block * row_block, row_block)
+
+            @pl.loop(0, width // LANES)
+            def _(unit, row=row):
+                attend_pair(
+                    qb, kb, vb, ob, row, row_block, first + unit * LANES, head_width
+                )
+
+            @pl.loop(0 if at < blocks else 1, owners)
+            def _(step, block=block):
+                target = block * owners + lax.rem(me + step, owners)
+                returned(chunk, target).start()
+
+        own_return(chunk).start()
 
     def arrive(chunk):
         turn, start, width = chunks[chunk]
@@ -931,13 +940,6 @@
             buffer = inputs[index][1]
             first = turn * cols + start
             take(recv_sem.at[index, chunk], buffer.at[:, first : first + width])
-
-    def give_back(chunk):
-        own_return(chunk).start()
-
-        @pl.loop(1, n)
-        def _(step):
-            returned(chunk, lax.rem(me + step, n)).start()
 
     def project(chunk):
         if chunk == 0:
@@ -1025,7 +1027,7 @@
             )
 
     actions = {
-        "issue": issue, "arrive": arrive, "attend": attend, "return": give_back,
+        "issue": issue, "arrive": arrive, "attend": attend,
         "line": line_step, "fan": fan_step, "group": group_step, "start": lambda _: line_start(),
         "project": project, "embed": embed, "judge": judge,
     }
@@ -1117,7 +1119,7 @@
         elif chunk == 0:
             steps += [("line", step) for step in lines[:1]] + [("fan", step) for step in fans[:1]]
             lines, fans = lines[1:], fans[1:]
-        steps += [("arrive", chunk), ("attend", chunk), ("return", chunk)]
+        steps += [("arrive", chunk), ("attend", chunk)]
         if chunk + 2 < count:
             steps.append(("issue", chunk + 2))
         if chunk < count - 1:
@@ -1260,6 +1262,8 @@
     particles, tokens, model_width = queries.shape
     if 2 * (model_width // HEADS) != LANES or not round_count(n, particles, model_width):
         return False
+    if 256 % tokens or n * tokens % 256:
+        return False
     return model_width % 512 == 0 and embed_weight.shape[1] % 512 == 0
 
 

time: 103 us -> 103 us (level)
  no operation moved by 1% of the time
where the time goes in v5:
time: 103 us
  Pallas kernels  100 us (97%)
  local copies, waits for them, and re-layouts  1.39 us (1%)
  between operations  1.29 us (1%)
    pallas_call x1, Pallas kernels, fused(): pl.pallas_call(functools.partial(fused_kernel, n, fan, group_count, dom_c...  100 us

profile of v5, /device:TPU:0, one launch (start us, length us, event | category | flops | bytes accessed | tf_op | source)
XLA Modules:
  0.0 102.8 jit_solution(1600404495717630367)
XLA Ops:
  1.3 100.2 %step.1 = (bf16[4,64,1536]{2,1,0:T(8,128)(2,1)S(1)}, f32[1,4]{1,0:T(1,128)S(1)}) custom-call(bf16[4,64,1536]{2,1,0:T(8,128)(2,1)} %q_ref.1, bf16[4,64,1536]{2,1,0:T(8,128)(2,1)} %k_ref.1, bf16[4,64,1536]{2,1,0:T(8,128)(2,1)} %v_ref.1, bf16[4,64,1536]{2,1,0:T(8,128)(2,1)} %lat_ref.1, bf16[1536,1536]{1,0:T(8,128)(2,1)} %wo_ref.1, s32[1]{0:T(128)S(6)} %copy.16.step_in, ...), custom_call_target="tpu_custom_call" | custom-call | tf_op jit(solution)/shard_map/step/pallas_call | solution.py:1176
  101.5 0.9 copy.17
  102.3 0.5 copy.18

commit v6 on v5

--- a/solution.py
+++ b/solution.py
@@ -1116,6 +1116,7 @@
             steps += [("line", step) for step in lines] + [("fan", step) for step in fans]
             steps += [("group", step) for step in range(length)]
             steps += [("project", part) for part in early]
+            steps += [("embed", turn) for turn in range(last)]
         elif chunk == 0:
             steps += [("line", step) for step in lines[:1]] + [("fan", step) for step in fans[:1]]
             lines, fans = lines[1:], fans[1:]
@@ -1126,7 +1127,7 @@
             steps += [("line", step) for step in lines[:1]] + [("fan", step) for step in fans[:1]]
             lines, fans = lines[1:], fans[1:]
     for turn in range(last):
-        steps += [("embed", turn), ("judge", turn)]
+        steps.append(("judge", turn))
     return steps + [("project", part) for part in late] + [("embed", last), ("judge", last)]
 
 

time: 103 us -> 103 us (level)
  no operation moved by 1% of the time
where the time goes in v6:
time: 103 us; the launch traced here: 102 us
  Pallas kernels  99.7 us (97%)
  local copies, waits for them, and re-layouts  1.39 us (1%)
  between operations  1.29 us (1%)
    pallas_call x1, Pallas kernels, fused(): pl.pallas_call(functools.partial(fused_kernel, n, fan, group_count, dom_c...  99.7 us

profile of v6, /device:TPU:0, one launch (start us, length us, event | category | flops | bytes accessed | tf_op | source)
XLA Modules:
  0.0 102.4 jit_solution(7108955628348974790)
XLA Ops:
  1.3 99.7 %step.1 = (bf16[4,64,1536]{2,1,0:T(8,128)(2,1)S(1)}, f32[1,4]{1,0:T(1,128)S(1)}) custom-call(bf16[4,64,1536]{2,1,0:T(8,128)(2,1)} %q_ref.1, bf16[4,64,1536]{2,1,0:T(8,128)(2,1)} %k_ref.1, bf16[4,64,1536]{2,1,0:T(8,128)(2,1)} %v_ref.1, bf16[4,64,1536]{2,1,0:T(8,128)(2,1)} %lat_ref.1, bf16[1536,1536]{1,0:T(8,128)(2,1)} %wo_ref.1, s32[1]{0:T(128)S(6)} %copy.16.step_in, ...), custom_call_target="tpu_custom_call" | custom-call | tf_op jit(solution)/shard_map/step/pallas_call | solution.py:1177
  101.0 0.9 copy.17
  101.9 0.5 copy.18
